TPU v7x, 32 devices: a whole 2x2x4 slice. The times are simulated.
32 devices in a mesh: outer: 4 (over y, core), inner: 8 (over z, x).
Axes of the slice: x: 2, y: 2, z: 4, core: 2. Of those that a mesh axis runs over, the one named last changes fastest.
Arguments:
- queries: bfloat16 [16384, 16, 128], P(('outer', 'inner')), may hold values from -1.5 to 1.5
- key_vectors: bfloat16 [16384, 16, 128], P(('outer', 'inner')), may hold values from -1.5 to 1.5
- value_vectors: bfloat16 [16384, 16, 128], P(('outer', 'inner')), may hold values from -6 to 6
- level_weights: float32 [18, 16, 16384], P(None, None, ('outer', 'inner')), may hold values from 0.25 to 1
Outputs:
- attended: bfloat16 [16384, 16, 128], P(('outer', 'inner'))
All inputs are finite; a program needn't handle non-finite values.
Results may differ from a plain program's by a relative error of at most 0.0049.
Values may be sent and summed in bfloat16 or wider, within the bound.
No kernel may reach another device: no remote copies, remote signals or barrier semaphores. Data moves between devices by JAX's collectives and lax.ppermute only.
A program may use at most 128 MiB of HBM per device.

v0:
```python
import jax
import jax.numpy as jnp
from jax import lax
from jax.sharding import PartitionSpec as P


def swapped(value, axis, distance):
    return lax.ppermute(value, axis, [(i, i ^ 1 << distance) for i in range(lax.axis_size(axis))])


def level_table(block_len):
    position = jnp.arange(block_len, dtype=jnp.int32)
    differ = position[:, None] ^ position[None, :]
    levels_at = jnp.zeros((block_len, block_len), jnp.int32)
    for bit_pos in range(block_len.bit_length() - 1):
        levels_at = levels_at + (differ >= 1 << bit_pos).astype(jnp.int32)
    causal = position[None, :] <= position[:, None]
    return (levels_at, causal)


def scaled_gains(level_weights):
    count = level_weights.shape[0]
    factor = jnp.exp2(-0.5 * jnp.arange(count, dtype=jnp.float32))
    return level_weights * factor[:, None, None]


def local_terms(queries, key_vectors, value_vectors, gains):
    block_len = queries.shape[0]
    levels_at, causal = level_table(block_len)
    scores = jnp.einsum("thd,shd->hts", queries, key_vectors, preferred_element_type=jnp.float32)
    weighting = jnp.zeros(scores.shape, jnp.float32)
    for level_idx in range(block_len.bit_length()):
        weighting = weighting + jnp.where(
            (levels_at == level_idx)[None], gains[level_idx][:, :, None], jnp.float32(0.0)
        )
    attn_weights = jnp.where(causal[None], scores * weighting, jnp.float32(0.0)).astype(
        jnp.bfloat16
    )
    return jnp.einsum(
        "hts,shd->thd", attn_weights, value_vectors, preferred_element_type=jnp.float32
    )


def sibling_buckets(states, outer_place, outer_depth):
    picked = []
    tier_now = states
    for bit_pos in range(outer_depth):
        sibling = outer_place >> bit_pos ^ 1
        picked.append(
            lax.dynamic_index_in_dim(tier_now, sibling, 0, keepdims=False).astype(jnp.bfloat16)
        )
        if bit_pos + 1 < outer_depth:
            tier_now = tier_now[0::2] + tier_now[1::2]
    return picked


def per_device(queries, key_vectors, value_vectors, level_weights):
    inner_count = lax.axis_size("inner")
    inner_depth = inner_count.bit_length() - 1
    outer_depth = lax.axis_size("outer").bit_length() - 1
    outer_place = lax.axis_index("outer")
    place = outer_place * inner_count + lax.axis_index("inner")
    block_len = queries.shape[0]
    local_depth = block_len.bit_length() - 1
    gains = scaled_gains(level_weights)
    key_value = jnp.einsum(
        "shd,she->hde", key_vectors, value_vectors, preferred_element_type=jnp.float32
    )
    output_sum = local_terms(queries, key_vectors, value_vectors, gains)
    buckets = []
    running = key_value
    for bit_pos in range(inner_depth):
        partner = swapped(running, "inner", bit_pos)
        buckets.append(partner.astype(jnp.bfloat16))
        running = running + partner
    states = lax.all_gather(running[None], "outer", axis=0, tiled=True)
    buckets.extend(sibling_buckets(states, outer_place, outer_depth))
    count = len(buckets)
    switches = [(place >> bit_pos & 1).astype(jnp.float32) for bit_pos in range(count)]
    for bit_pos in range(count):
        contrib = jnp.einsum(
            "thd,hde->the", queries, buckets[bit_pos], preferred_element_type=jnp.float32
        )
        level_gain = gains[local_depth + 1 + bit_pos] * switches[bit_pos]
        output_sum = output_sum + contrib * level_gain.T[:, :, None]
    return output_sum.astype(jnp.bfloat16)


def solution(mesh):
    placed = (
        P(("outer", "inner"), None, None),
        P(("outer", "inner"), None, None),
        P(("outer", "inner"), None, None),
        P(None, None, ("outer", "inner")),
    )
    return jax.shard_map(
        per_device,
        mesh=mesh,
        in_specs=placed,
        out_specs=P(("outer", "inner"), None, None),
        check_vma=False,
    )
```

profile of v0, /device:TPU:0, one launch (start us, length us, event | category | flops | bytes accessed | tf_op | source)
XLA Modules:
  0.0 181.2 jit_solution(11538674731520558724)
XLA Ops:
  6.5 0.0 copy-start
  6.5 0.0 all-gather.3.cloned.1.call-start
  6.5 4.4 %copy.26 = bf16[512,16,128]{0,2,1:T(8,128)(2,1)} copy(bf16[512,16,128]{2,1,0:T(8,128)(2,1)} %param.5) | data formatting | bytes 4194304 | tf_op args[1]
  11.0 0.0 copy-done
  11.0 2.7 %fusion.7 = f32[16,128,128]{2,1,0:T(8,128)S(1)} fusion(bf16[512,16,128]{0,2,1:T(8,128)(2,1)} %copy.26, bf16[512,16,128]{2,1,0:T(8,128)(2,1)S(1)} %copy-done), kind=kOutput, calls=%fused_computation.13 | convolution fusion | flops 268435456 | bytes 5242880 | tf_op jit(solution)/shard_map/shd,she->hde/dot_general | solution.py:66
  13.7 3.0 %collective-permute-start = (f32[16,128,128]{2,1,0:T(8,128)S(1)}, f32[16,128,128]{2,1,0:T(8,128)S(1)}, u32[]{:S(2)}, u32[]{:S(2)}) collective-permute-start(f32[16,128,128]{2,1,0:T(8,128)S(1)} %fusion.7), channel_id=1, source_target_pairs={{0,1},{1,0},{2,3},{3,2},{4,5},{5,4},{6,7},{7,6},{8,9},{9,8},{10,11... | collective-permute-start | bytes 3145736 | tf_op jit(solution)/shard_map/ppermute | solution.py:8
  16.7 23.2 %collective-permute-done = f32[16,128,128]{2,1,0:T(8,128)S(1)} collective-permute-done((f32[16,128,128]{2,1,0:T(8,128)S(1)}, f32[16,128,128]{2,1,0:T(8,128)S(1)}, u32[]{:S(2)}, u32[]{:S(2)}) %collective-permute-start) | collective-permute-done | bytes 1048608 | tf_op jit(solution)/shard_map/ppermute | solution.py:8
  39.9 0.1 add.500
  40.0 1.9 %collective-permute-start.1 = (f32[16,128,128]{2,1,0:T(8,128)S(1)}, f32[16,128,128]{2,1,0:T(8,128)S(1)}, u32[]{:S(2)}, u32[]{:S(2)}) collective-permute-start(f32[16,128,128]{2,1,0:T(8,128)S(1)} %add.500), channel_id=1, source_target_pairs={{0,2},{1,3},{2,0},{3,1},{4,6},{5,7},{6,4},{7,5},{8,10},{9,11},{10,... | collective-permute-start | bytes 3145736 | tf_op jit(solution)/shard_map/ppermute | solution.py:8
  41.9 22.5 %collective-permute-done.1 = f32[16,128,128]{2,1,0:T(8,128)S(1)} collective-permute-done((f32[16,128,128]{2,1,0:T(8,128)S(1)}, f32[16,128,128]{2,1,0:T(8,128)S(1)}, u32[]{:S(2)}, u32[]{:S(2)}) %collective-permute-start.1) | collective-permute-done | bytes 1048608 | tf_op jit(solution)/shard_map/ppermute | solution.py:8
  64.4 0.0 copy-done.6
  64.4 1.3 add.502
  65.7 0.1 copy-done.8
  65.9 2.6 %collective-permute-start.2 = (f32[16,128,128]{2,1,0:T(8,128)}, f32[16,128,128]{2,1,0:T(8,128)S(1)}, u32[]{:S(2)}, u32[]{:S(2)}) collective-permute-start(f32[16,128,128]{2,1,0:T(8,128)} %add.502), channel_id=1, source_target_pairs={{0,4},{1,5},{2,6},{3,7},{4,0},{5,1},{6,2},{7,3},{8,12},{9,13},{10,... | collective-permute-start | bytes 3145736 | tf_op jit(solution)/shard_map/ppermute | solution.py:8
  68.4 1.0 iota_compare_fusion
  69.4 1.2 broadcast_compare_fusion.1
  70.6 1.1 broadcast_compare_fusion.3
  71.8 1.1 broadcast_compare_fusion.5
  72.9 1.1 broadcast_compare_fusion.7
  74.0 38.9 %collective-permute-done.2 = f32[16,128,128]{2,1,0:T(8,128)S(1)} collective-permute-done((f32[16,128,128]{2,1,0:T(8,128)}, f32[16,128,128]{2,1,0:T(8,128)S(1)}, u32[]{:S(2)}, u32[]{:S(2)}) %collective-permute-start.2) | collective-permute-done | bytes 1048608 | tf_op jit(solution)/shard_map/ppermute | solution.py:8
  112.9 2.4 %add.504 = f32[16,128,128]{2,1,0:T(8,128)} add(f32[16,128,128]{2,1,0:T(8,128)} %add.502, f32[16,128,128]{2,1,0:T(8,128)S(1)} %collective-permute-done.2) | non-fusion elementwise | flops 262144 | bytes 3145728 | tf_op jit(solution)/shard_map/add | solution.py:75
  115.2 0.0 all-gather.3.cloned.1.call-update
  115.3 0.3 broadcast_compare_fusion.9
  115.5 1.2 broadcast_multiply_fusion
  116.7 0.7 fusion.42
  117.4 22.4 %select_convert_fusion.clone.4 = bf16[16,512,512]{2,1,0:T(8,128)(2,1)S(1)} fusion(bf16[512,16,128]{0,2,1:T(8,128)(2,1)} %copy.26, f32[16,512]{1,0:T(8,128)S(1)} %get-tuple-element.12, f32[16,512]{1,0:T(8,128)S(1)} %get-tuple-element.13, f32[16,512]{1,0:T(8,128)S(1)} %get-tuple-element.14, f32[16,512]{1,0:T(8,128)S(1)} %get-tuple-element.15, ...), kind=kOutput, calls=%fused_computation.clone.clone.clone.1 | convolution fusion | flops 1166016512 | bytes 15794176 | tf_op jit(solution)/shard_map/thd,shd->hts/dot_general | solution.py:30
  139.8 0.0 copy-start.1
  139.8 0.0 copy-start.7
  139.8 4.4 %fusion.6 = f32[16,512,128]{2,1,0:T(8,128)} fusion(bf16[512,16,128]{2,1,0:T(8,128)(2,1)S(1)} %copy-done, bf16[16,512,512]{2,1,0:T(8,128)(2,1)S(1)} %select_convert_fusion.clone.4), kind=kOutput, calls=%fused_computation.12 | convolution fusion | flops 1073741824 | bytes 14680064 | tf_op jit(solution)/shard_map/hts,shd->thd/dot_general | solution.py:39
  144.2 0.0 copy-done.1
  144.2 0.0 copy-done.7
  144.2 2.7 %fusion.22 = f32[16,128,512]{1,2,0:T(8,128)} fusion(bf16[512,16,128]{2,1,0:T(8,128)(2,1)S(1)} %copy-done.1, f32[16,128,128]{2,1,0:T(8,128)S(1)} %copy-done.7), kind=kOutput, calls=%fused_computation.33 | convolution fusion | flops 268697600 | bytes 7340032 | tf_op jit(solution)/shard_map/thd,hde->the/dot_general | solution.py:81
  146.9 0.0 copy-done.9
  146.9 2.7 %fusion.24 = f32[16,128,512]{1,2,0:T(8,128)} fusion(bf16[512,16,128]{2,1,0:T(8,128)(2,1)S(1)} %copy-done.1, f32[16,128,128]{2,1,0:T(8,128)S(1)} %copy-done.9), kind=kOutput, calls=%fused_computation.35 | convolution fusion | flops 268697600 | bytes 7340032 | tf_op jit(solution)/shard_map/thd,hde->the/dot_general | solution.py:81
  149.5 1.2 all-gather.3.cloned.1.call-done
  150.7 5.6 %copy.37 = f32[64,128,128]{1,2,0:T(8,128)} copy(f32[64,128,128]{2,1,0:T(8,128)} %all-gather.3.cloned.1.call-done) | data formatting | bytes 8388608 | tf_op jit(solution)/shard_map/all_gather | solution.py:76
  156.3 2.6 %fusion.46 = (f32[2,16,128,128]{2,3,1,0:T(8,128)S(1)}, f32[2,16,128,128]{2,3,1,0:T(8,128)S(1)}) fusion(f32[4,16,128,128]{2,3,1,0:T(8,128)} %bitcast.85), kind=kLoop, calls=%fused_computation.81 | loop fusion | bytes 8388608 | tf_op jit(solution)/shard_map/slice | solution.py:53
  159.0 0.2 copy-done.2
  159.2 2.1 %fusion.29 = f32[16,128,512]{1,2,0:T(8,128)S(1)} fusion(bf16[512,16,128]{2,1,0:T(8,128)(2,1)S(1)} %copy-done.2, f32[4,16,128,128]{2,3,1,0:T(8,128)} %bitcast.86, s32[]{:T(128)S(6)} %select_n.54), kind=kOutput, calls=%fused_computation.39 | convolution fusion | flops 268435456 | bytes 6815748 | tf_op jit(solution)/shard_map/thd,hde->the/dot_general | solution.py:81
  161.3 0.0 copy-start.3
  161.3 0.0 copy-start.4
  161.3 0.8 fusion.20
  162.1 0.0 copy-done.5
  162.1 0.0 copy-done.10
  162.1 1.5 copy-done.3
  163.6 1.2 copy-done.4
  164.8 6.9 %fusion.1 = bf16[512,16,128]{2,0,1:T(8,128)(2,1)S(1)} fusion(f32[16,128,512]{1,2,0:T(8,128)S(1)} %fusion.20, f32[16,128,512]{1,2,0:T(8,128)S(1)} %fusion.29, f32[16,128,512]{1,2,0:T(8,128)S(1)} %copy-done.5, f32[16,128,512]{1,2,0:T(8,128)S(1)} %copy-done.4, f32[16,512,128]{2,1,0:T(8,128)S(1)} %copy-done.3, f32[512,16]{0,1:T(8,128)S(1)} %get-tuple-element.8, ...), kind=kOutput, calls=%fused_computation.3 | convolution fusion | flops 280231936 | bytes 26378240 | tf_op jit(solution)/shard_map/thd,hde->the/dot_general | solution.py:81
  171.7 2.7 %copy.42 = bf16[512,16,128]{2,1,0:T(8,128)(2,1)} copy(bf16[512,16,128]{2,0,1:T(8,128)(2,1)S(1)} %fusion.1) | data formatting | bytes 4194304 | tf_op jit(solution)/shard_map/convert_element_type | solution.py:86
  (8 shorter events, 0.0 us)
Async XLA Ops:
  6.5 4.4 %copy-start = (bf16[512,16,128]{2,1,0:T(8,128)(2,1)S(1)}, bf16[512,16,128]{2,1,0:T(8,128)(2,1)}, u32[]{:S(2)}) copy-start(bf16[512,16,128]{2,1,0:T(8,128)(2,1)} %param.6) | copy-start | bytes 6291460
  6.5 144.2 %all-gather.3.cloned.1.call-start = ((), (), s32[]{:S(2)}) async-start(), calls=%async_computation | async-start | bytes 5242880 | tf_op jit(solution)/shard_map/all_gather | solution.py:76
  13.7 26.2 %collective-permute-start = (f32[16,128,128]{2,1,0:T(8,128)S(1)}, f32[16,128,128]{2,1,0:T(8,128)S(1)}, u32[]{:S(2)}, u32[]{:S(2)}) collective-permute-start(f32[16,128,128]{2,1,0:T(8,128)S(1)} %fusion.7), channel_id=1, source_target_pairs={{0,1},{1,0},{2,3},{3,2},{4,5},{5,4},{6,7},{7,6},{8,9},{9,8},{10,11... | collective-permute-start | bytes 3145736 | tf_op jit(solution)/shard_map/ppermute | solution.py:8
  39.9 24.5 %copy-start.6 = (f32[16,128,128]{2,1,0:T(8,128)}, f32[16,128,128]{2,1,0:T(8,128)S(1)}, u32[]{:S(2)}) copy-start(f32[16,128,128]{2,1,0:T(8,128)S(1)} %collective-permute-done) | copy-start | bytes 3145732
  40.0 24.4 %collective-permute-start.1 = (f32[16,128,128]{2,1,0:T(8,128)S(1)}, f32[16,128,128]{2,1,0:T(8,128)S(1)}, u32[]{:S(2)}, u32[]{:S(2)}) collective-permute-start(f32[16,128,128]{2,1,0:T(8,128)S(1)} %add.500), channel_id=1, source_target_pairs={{0,2},{1,3},{2,0},{3,1},{4,6},{5,7},{6,4},{7,5},{8,10},{9,11},{10,... | collective-permute-start | bytes 3145736 | tf_op jit(solution)/shard_map/ppermute | solution.py:8
  64.4 1.4 copy-start.8
  65.9 47.0 %collective-permute-start.2 = (f32[16,128,128]{2,1,0:T(8,128)}, f32[16,128,128]{2,1,0:T(8,128)S(1)}, u32[]{:S(2)}, u32[]{:S(2)}) collective-permute-start(f32[16,128,128]{2,1,0:T(8,128)} %add.502), channel_id=1, source_target_pairs={{0,4},{1,5},{2,6},{3,7},{4,0},{5,1},{6,2},{7,3},{8,12},{9,13},{10,... | collective-permute-start | bytes 3145736 | tf_op jit(solution)/shard_map/ppermute | solution.py:8
  139.8 4.4 %copy-start.1 = (bf16[512,16,128]{2,1,0:T(8,128)(2,1)S(1)}, bf16[512,16,128]{2,1,0:T(8,128)(2,1)}, u32[]{:S(2)}) copy-start(bf16[512,16,128]{2,1,0:T(8,128)(2,1)} %param.4) | copy-start | bytes 6291460
  139.8 4.4 %copy-start.7 = (f32[16,128,128]{2,1,0:T(8,128)S(1)}, f32[16,128,128]{2,1,0:T(8,128)}, u32[]{:S(2)}) copy-start(f32[16,128,128]{2,1,0:T(8,128)} %copy-done.6) | copy-start | bytes 3145732
  144.2 2.7 %copy-start.9 = (f32[16,128,128]{2,1,0:T(8,128)S(1)}, f32[16,128,128]{2,1,0:T(8,128)}, u32[]{:S(2)}) copy-start(f32[16,128,128]{2,1,0:T(8,128)} %copy-done.8) | copy-start | bytes 3145732
  156.3 2.9 %copy-start.2 = (bf16[512,16,128]{2,1,0:T(8,128)(2,1)S(1)}, bf16[512,16,128]{2,1,0:T(8,128)(2,1)}, u32[]{:S(2)}) copy-start(bf16[512,16,128]{2,1,0:T(8,128)(2,1)} %param.4) | copy-start | bytes 6291460
  159.2 2.9 %copy-start.5 = (f32[16,128,512]{1,2,0:T(8,128)S(1)}, f32[16,128,512]{1,2,0:T(8,128)}, u32[]{:S(2)}) copy-start(f32[16,128,512]{1,2,0:T(8,128)} %fusion.24) | copy-start | bytes 12582916
  159.2 2.9 %copy-start.10 = (f32[512,16]{0,1:T(8,128)S(1)}, f32[512,16]{0,1:T(8,128)}, u32[]{:S(2)}) copy-start(f32[512,16]{0,1:T(8,128)} %get-tuple-element.11) | copy-start | bytes 98308
  161.3 2.3 %copy-start.3 = (f32[16,512,128]{2,1,0:T(8,128)S(1)}, f32[16,512,128]{2,1,0:T(8,128)}, u32[]{:S(2)}) copy-start(f32[16,512,128]{2,1,0:T(8,128)} %fusion.6) | copy-start | bytes 12582916
  161.3 3.5 %copy-start.4 = (f32[16,128,512]{1,2,0:T(8,128)S(1)}, f32[16,128,512]{1,2,0:T(8,128)}, u32[]{:S(2)}) copy-start(f32[16,128,512]{1,2,0:T(8,128)} %fusion.22) | copy-start | bytes 12582916
Sparse Core Ops, SparseCore 0:
  115.4 35.2 all-gather.2
where the time goes:
time: 182 us; the launch traced here: 181 us
  waiting for transfers between devices  85.7 us (47%)
  matrix products  44.6 us (25%)
  local copies, waits for them, and re-layouts  18.4 us (10%)
  between operations  13.5 us (7%)
  other arithmetic  11.4 us (6%)
  starting transfers between devices  7.49 us (4%)
    ppermute x3, waiting for transfers between devices, swapped(): lax.ppermute(value, axis, [(i, i ^ 1 << distance) for i in range(lax.axis...  84.5 us
    dot_general x1, matrix products, local_terms(): jnp.einsum('thd,shd->hts', queries, key_vectors, preferred_element_type=j...  22.4 us
    dot_general x5, matrix products, per_device(): jnp.einsum('thd,hde->the', queries, buckets[bit_pos], preferred_element_t...  15.1 us
    ppermute x3, starting transfers between devices, swapped(): lax.ppermute(value, axis, [(i, i ^ 1 << distance) for i in range(lax.axis...  7.49 us
    unnamed x23, local copies, waits for them, and re-layouts  7.48 us
    all_gather x1, local copies, waits for them, and re-layouts, per_device(): states = lax.all_gather(running[None], 'outer', axis=0, tiled=True)  5.59 us
    eq x5, other arithmetic, local_terms(): levels_at == level_idx  4.81 us
    dot_general x1, matrix products, local_terms(): jnp.einsum('hts,shd->thd', attn_weights, value_vectors, preferred_element...  4.36 us
  transfers between devices with their start and end apart: 4, of which 4 were waited for; matrix products, arithmetic and copies ran while one was open for 22% of the time, Pallas kernels for 0%

commit v1 on v0

v1 whole, which is shorter than its diff:
```python
import functools
import jax
import jax.numpy as jnp
from jax import lax
from jax.experimental import pallas as pl
from jax.sharding import PartitionSpec as P

AXES = ("outer", "inner")
HEAD_BLOCK = 8
F32, BF16 = jnp.float32, jnp.bfloat16


def dot_nt(a, b):
    return lax.dot_general(a, b, (((1,), (1,)), ((), ())), preferred_element_type=F32)


def state_kernel(k_ref, v_ref, state_ref, first_ref):
    half = k_ref.shape[0] // 2
    keys = jnp.swapaxes(k_ref[...], 0, 1)
    values = jnp.swapaxes(v_ref[...], 0, 1)
    for h in range(keys.shape[0]):
        turned = values[h].T
        first = jnp.dot(turned[:, :half], keys[h, :half], preferred_element_type=F32)
        rest = jnp.dot(turned[:, half:], keys[h, half:], preferred_element_type=F32)
        first_ref[h] = first.astype(BF16)
        state_ref[h] = (first + rest).astype(BF16)


def block_states(key_vectors, value_vectors):
    tokens, heads, dim = key_vectors.shape
    source = pl.BlockSpec((tokens, HEAD_BLOCK, dim), lambda i: (0, i, 0))
    target = pl.BlockSpec((HEAD_BLOCK, dim, dim), lambda i: (i, 0, 0))
    shape = jax.ShapeDtypeStruct((heads, dim, dim), BF16)
    return pl.pallas_call(
        state_kernel,
        grid=(heads // HEAD_BLOCK,),
        in_specs=[source, source],
        out_specs=[target, target],
        out_shape=[shape, shape],
        name="states",
        cost_estimate=pl.CostEstimate(
            flops=2 * tokens * heads * dim * dim,
            bytes_accessed=4 * tokens * heads * dim,
            transcendentals=0,
        ),
    )(key_vectors, value_vectors)


def local_kernel(second, q_ref, k_ref, v_ref, w_ref, first_ref, acc_ref, qh_ref):
    tile = q_ref.shape[0]
    depth = tile.bit_length() - 1
    groups = tile // 8
    queries = jnp.swapaxes(q_ref[...], 0, 1)
    keys = jnp.swapaxes(k_ref[...], 0, 1)
    values = jnp.swapaxes(v_ref[...], 0, 1)
    lane = lax.broadcasted_iota(jnp.int32, (8, tile), 1)
    row = lax.broadcasted_iota(jnp.int32, (8, tile), 0)
    fine = (lane & 7) ^ row
    fine_ok = row <= (lane & 7)
    group_lane = lax.broadcasted_iota(jnp.int32, (groups, tile), 1) >> 3
    group_row = lax.broadcasted_iota(jnp.int32, (groups, tile), 0)
    coarse = jnp.where(group_row < group_lane, group_lane ^ group_row, 0)
    for h in range(queries.shape[0]):
        gain = [w_ref[l, h : h + 1, :] * (2.0 ** (-0.5 * l)) for l in range(depth + 2)]
        near = jnp.where(fine == 0, gain[0], 0.0)
        for l in range(1, 4):
            near = jnp.where((fine >> (l - 1)) == 1, gain[l], near)
        near = jnp.where(fine_ok, near, 0.0)
        far = jnp.zeros((groups, tile), F32)
        for l in range(4, depth + 1):
            far = jnp.where((coarse >> (l - 4)) == 1, gain[l], far)
        scores = dot_nt(keys[h], queries[h])
        rows = []
        for g in range(0, groups, 2):
            pair = [
                jnp.where(
                    (lane >> 3) == g + i,
                    near,
                    jnp.broadcast_to(far[g + i : g + i + 1, :], (8, tile)),
                )
                * scores[8 * (g + i) : 8 * (g + i) + 8, :]
                for i in range(2)
            ]
            rows.append(jnp.concatenate(pair, axis=0).astype(BF16))
        weights = jnp.concatenate(rows, axis=0)
        out = jnp.dot(values[h].T, weights, preferred_element_type=F32)
        if second:
            out = out + gain[depth + 1] * dot_nt(first_ref[h], queries[h])
        acc_ref[h] = out
        qh_ref[h] = queries[h]


def local_part(half, queries, key_vectors, value_vectors, level_weights, first):
    tokens, heads, dim = queries.shape
    tile = tokens // 2
    levels = tile.bit_length() + 1
    source = pl.BlockSpec((tile, HEAD_BLOCK, dim), lambda i: (half, i, 0))
    return pl.pallas_call(
        functools.partial(local_kernel, half == 1),
        grid=(heads // HEAD_BLOCK,),
        in_specs=[
            source,
            source,
            source,
            pl.BlockSpec((levels, HEAD_BLOCK, tile), lambda i: (0, i, half)),
            pl.BlockSpec((HEAD_BLOCK, dim, dim), lambda i: (i, 0, 0)),
        ],
        out_specs=[
            pl.BlockSpec((HEAD_BLOCK, dim, tile), lambda i: (i, 0, 0)),
            pl.BlockSpec((HEAD_BLOCK, tile, dim), lambda i: (i, 0, 0)),
        ],
        out_shape=[
            jax.ShapeDtypeStruct((heads, dim, tile), F32),
            jax.ShapeDtypeStruct((heads, tile, dim), BF16),
        ],
        cost_estimate=pl.CostEstimate(
            flops=4 * tile * tile * heads * dim,
            bytes_accessed=12 * tile * heads * dim,
            transcendentals=0,
        ),
    )(queries, key_vectors, value_vectors, level_weights, first)


def merge_kernel(count, qh_ref, acc_ref, w_ref, *rest):
    out_ref = rest[count]
    for h in range(qh_ref.shape[0]):
        total = acc_ref[h]
        for n in range(count):
            total = total + w_ref[n, h : h + 1, :] * dot_nt(rest[n][h], qh_ref[h])
        out_ref[h] = total


def merge_part(half, turned, acc, gains, buckets):
    heads, tile, dim = turned.shape
    count = len(buckets)
    return pl.pallas_call(
        functools.partial(merge_kernel, count),
        grid=(heads // HEAD_BLOCK,),
        in_specs=[
            pl.BlockSpec((HEAD_BLOCK, tile, dim), lambda i: (i, 0, 0)),
            pl.BlockSpec((HEAD_BLOCK, dim, tile), lambda i: (i, 0, 0)),
            pl.BlockSpec((count, HEAD_BLOCK, tile), lambda i: (0, i, half)),
        ]
        + [pl.BlockSpec((HEAD_BLOCK, dim, dim), lambda i: (i, 0, 0))] * count,
        out_specs=pl.BlockSpec((HEAD_BLOCK, dim, tile), lambda i: (i, 0, 0)),
        out_shape=jax.ShapeDtypeStruct((heads, dim, tile), F32),
        input_output_aliases={1: 0},
        cost_estimate=pl.CostEstimate(
            flops=2 * count * tile * heads * dim * dim,
            bytes_accessed=10 * tile * heads * dim,
            transcendentals=0,
        ),
    )(turned, acc, gains, *buckets)


def final_kernel(count, q0_ref, q1_ref, a0_ref, a1_ref, w_ref, *rest):
    out_ref = rest[count]

    def side(q_ref, a_ref):
        done = []
        for h in range(q_ref.shape[0]):
            total = a_ref[h]
            for n in range(count):
                total = total + w_ref[n, h : h + 1, :] * dot_nt(rest[n][h], q_ref[h])
            done.append(total.T.astype(BF16))
        out_ref[...] = jnp.swapaxes(jnp.stack(done), 0, 1)

    which = pl.program_id(0)
    pl.when(which == 0)(lambda: side(q0_ref, a0_ref))
    pl.when(which == 1)(lambda: side(q1_ref, a1_ref))


def final_part(turned, accs, gains, buckets):
    heads, tile, dim = turned[0].shape
    count = len(buckets)
    blocks = heads // HEAD_BLOCK
    first = lambda s, i: (jnp.where(s == 0, i, blocks - 1), 0, 0)
    last = lambda s, i: (jnp.where(s == 1, i, 0), 0, 0)
    return pl.pallas_call(
        functools.partial(final_kernel, count),
        grid=(2, blocks),
        in_specs=[
            pl.BlockSpec((HEAD_BLOCK, tile, dim), first),
            pl.BlockSpec((HEAD_BLOCK, tile, dim), last),
            pl.BlockSpec((HEAD_BLOCK, dim, tile), first),
            pl.BlockSpec((HEAD_BLOCK, dim, tile), last),
            pl.BlockSpec((count, HEAD_BLOCK, tile), lambda s, i: (0, i, s)),
        ]
        + [pl.BlockSpec((HEAD_BLOCK, dim, dim), lambda s, i: (i, 0, 0))] * count,
        out_specs=pl.BlockSpec((tile, HEAD_BLOCK, dim), lambda s, i: (s, i, 0)),
        out_shape=jax.ShapeDtypeStruct((2 * tile, heads, dim), BF16),
        name="final",
        cost_estimate=pl.CostEstimate(
            flops=4 * count * tile * heads * dim * dim,
            bytes_accessed=16 * tile * heads * dim,
            transcendentals=0,
        ),
    )(*turned, *accs, gains, *buckets)


def exchange(value, mask, keep=None):
    total = lax.axis_size("outer") * lax.axis_size("inner")
    pairs = [(i, i ^ mask) for i in range(total) if keep is None or keep(i ^ mask)]
    return lax.ppermute(value, AXES, pairs)


def exchange_states(state, place, inner_depth, depth):
    quarter = state.shape[0] // 4
    rank = place & 3
    part = lambda r: lax.dynamic_slice_in_dim(state, r * quarter, quarter, 0)
    got = {m: exchange(part(rank ^ m), m) for m in (3, 2, 1)}
    buckets = {0: exchange(state, 1, lambda d: d & 1 == 1)}
    mine = part(rank).astype(F32) + got[1].astype(F32)
    other = got[2].astype(F32) + got[3].astype(F32)
    high, odd = (rank >> 1) == 1, (rank & 1) == 1
    pieces = {1: jnp.where(high, other, mine).astype(BF16)}
    total = mine + other
    for g in range(2, depth):
        pieces[g] = exchange(total.astype(BF16), 1 << g)
        total = total + pieces[g].astype(F32)

    def gather_late(g):
        a = pieces[g]
        b = exchange(a, 2)
        pair = jnp.stack([jnp.where(high, b, a), jnp.where(high, a, b)])
        twin = exchange(pair, 1)
        both = jnp.stack([jnp.where(odd, twin, pair), jnp.where(odd, pair, twin)], 1)
        return both.reshape(state.shape)

    low, top = inner_depth, depth - 1
    for g in range(1, depth):
        if g not in (low, top):
            buckets[g] = gather_late(g)
    upper = (place >> low & 1) == 1
    chosen = jnp.where(upper, pieces[low], pieces[top])
    full = jnp.zeros((4,) + chosen.shape, BF16)
    full = lax.dynamic_update_slice_in_dim(full, chosen[None], rank, 0)
    for m in (3, 2, 1):
        piece = exchange(chosen, m)
        full = lax.dynamic_update_slice_in_dim(full, piece[None], rank ^ m, 0)
    full = full.reshape(state.shape)
    handed = exchange(full, 1 << low, lambda d: d >> low & 1 == 1)
    buckets[low] = full
    buckets[top] = jnp.where(upper, handed, full)
    return [buckets[g] for g in range(depth)]


def per_device(queries, key_vectors, value_vectors, level_weights):
    inner_count = lax.axis_size("inner")
    inner_depth = inner_count.bit_length() - 1
    depth = inner_depth + lax.axis_size("outer").bit_length() - 1
    place = lax.axis_index("outer") * inner_count + lax.axis_index("inner")
    local_depth = queries.shape[0].bit_length() - 1
    state, first = block_states(key_vectors, value_vectors)
    buckets = exchange_states(state, place, inner_depth, depth)
    bits = jnp.arange(depth)
    factor = jnp.exp2(-0.5 * (local_depth + 1 + bits).astype(F32))
    factor = factor * (place >> bits & 1).astype(F32)
    gains = level_weights[local_depth + 1 : local_depth + 1 + depth] * factor[:, None, None]
    turned, accs = [], []
    late = (inner_depth, depth - 1)
    early = [g for g in range(depth) if g not in late]
    pick = lambda order: jnp.stack([gains[g] for g in order])
    for half in range(2):
        acc, flat = local_part(
            half, queries, key_vectors, value_vectors, level_weights, first
        )
        accs.append(merge_part(half, flat, acc, pick(early), [buckets[g] for g in early]))
        turned.append(flat)
    return final_part(turned, accs, pick(late), [buckets[g] for g in late])


def solution(mesh):
    placed = P(AXES, None, None)
    return jax.shard_map(
        per_device,
        mesh=mesh,
        in_specs=(placed, placed, placed, P(None, None, AXES)),
        out_specs=placed,
        check_vma=False,
    )
```

time: 182 us -> 73.6 us (0.40)
  waiting for transfers between devices: 85.7 us -> 13.8 us
  matrix products: 44.6 us -> 0 us
  Pallas kernels: 0 us -> 28.1 us
  starting transfers between devices: 7.49 us -> 22.9 us
  local copies, waits for them, and re-layouts: 18.4 us -> 4.97 us
  between operations: 13.5 us -> 0.16 us
  other arithmetic: 11.4 us -> 3.32 us
    ppermute x3 -> x15, waiting for transfers between devices: 84.5 us -> 13.8 us  [exchange(): return lax.ppermute(value, AXES, pairs)]
    dot_general x8 -> x0, matrix products: 44.6 us -> none  [the longest x1 22.4 us: local_terms(): jnp.einsum('thd,shd->hts', queries, key_vectors, preferred_element_type=j...]
    pallas_call x0 -> x6, Pallas kernels: none -> 28.1 us  [the longest x2 10.7 us: local_part(): pl.pallas_call(functools.partial(local_kernel, half == 1), grid=(heads //...]
    ppermute x3 -> x15, starting transfers between devices: 7.49 us -> 22.9 us  [exchange(): return lax.ppermute(value, AXES, pairs)]
    unnamed x23 -> x4, local copies, waits for them, and re-layouts: 7.48 us -> 0.8 us
    all_gather x1 -> x0, local copies, waits for them, and re-layouts: 5.59 us -> none  [per_device(): states = lax.all_gather(running[None], 'outer', axis=0, tiled=True)]
    eq x5 -> x0, other arithmetic: 4.81 us -> none  [local_terms(): levels_at == level_idx]
    add x3 -> x0, other arithmetic: 3.77 us -> none  [per_device(): running = running + partner]
  transfers between devices with their start and end apart: 4 -> 15, of which waited for: 4 -> 7; matrix products, arithmetic and copies ran while one was open for 22% -> 8% of each run, Pallas kernels for 0% -> 25%
where the time goes in v1:
time: 73.6 us; the launch traced here: 73.3 us
  Pallas kernels  28.1 us (38%)
  starting transfers between devices  22.9 us (31%)
  waiting for transfers between devices  13.8 us (19%)
  local copies, waits for them, and re-layouts  4.97 us (7%)
  other arithmetic  3.32 us (5%)
    ppermute x15, starting transfers between devices, exchange(): return lax.ppermute(value, AXES, pairs)  22.9 us
    ppermute x15, waiting for transfers between devices, exchange(): return lax.ppermute(value, AXES, pairs)  13.8 us
    pallas_call x2, Pallas kernels, local_part(): pl.pallas_call(functools.partial(local_kernel, half == 1), grid=(heads //...  10.7 us
    pallas_call x2, Pallas kernels, merge_part(): pl.pallas_call(functools.partial(merge_kernel, count), grid=(heads // HEA...  7.73 us
    pallas_call x1, Pallas kernels, final_part(): pl.pallas_call(functools.partial(final_kernel, count), grid=(2, blocks),...  6.19 us
    pallas_call x1, Pallas kernels, block_states(): pl.pallas_call(state_kernel, grid=(heads // HEAD_BLOCK,), in_specs=[sourc...  3.53 us
    another operation x2, local copies, waits for them, and re-layouts, gather_late(): jnp.stack([jnp.where(odd, twin, pair), jnp.where(odd, pair, twin)], 1)  1.67 us
  transfers between devices with their start and end apart: 15, of which 7 were waited for; matrix products, arithmetic and copies ran while one was open for 8% of the time, Pallas kernels for 25%

profile of v1, /device:TPU:0, one launch (start us, length us, event | category | flops | bytes accessed | tf_op | source)
XLA Modules:
  0.0 73.3 jit_solution(12093796800574832033)
XLA Ops:
  0.0 3.5 %states.1 = (bf16[16,128,128]{2,1,0:T(8,128)(2,1)}, bf16[16,128,128]{2,1,0:T(8,128)(2,1)}) custom-call(bf16[512,16,128]{2,1,0:T(8,128)(2,1)} %k_ref.5, bf16[512,16,128]{2,1,0:T(8,128)(2,1)} %v_ref.5), custom_call_target="tpu_custom_call" | custom-call | flops 268435456 | bytes 4194304 | tf_op jit(solution)/shard_map/states/pallas_call | solution.py:34
  3.5 1.1 %constant_dynamic-slice_fusion = (bf16[4,128,128]{2,1,0:T(8,128)(2,1)S(1)}, bf16[4,128,128]{2,1,0:T(8,128)(2,1)S(1)}, bf16[4,128,128]{2,1,0:T(8,128)(2,1)S(1)}) fusion(bf16[16,128,128]{2,1,0:T(8,128)(2,1)} %get-tuple-element.15, s32[]{:T(128)S(6)} %select_n.89, s32[]{:T(128)S(6)} %select_n.87, s32[]{:T(128)S(6)} %select_n.86), kind=kLoop, calls=%fused_computation.26 | loop fusion | bytes 786444 | tf_op jit(solution)/shard_map/dynamic_slice | solution.py:210
  4.6 4.0 %collective-permute-start.2 = (bf16[4,128,128]{2,1,0:T(8,128)(2,1)S(1)}, bf16[4,128,128]{2,1,0:T(8,128)(2,1)S(1)}, u32[]{:S(2)}, u32[]{:S(2)}) collective-permute-start(bf16[4,128,128]{2,1,0:T(8,128)(2,1)S(1)} %get-tuple-element.27), channel_id=1, source_target_pairs={{0,3},{1,2},{2,1},{3,0},{4,7},{5,6},{6,5},{7,4},{8,11},{9,10},{10,... | collective-permute-start | bytes 393224 | tf_op jit(solution)/shard_map/ppermute | solution.py:204
  8.6 0.4 collective-permute-start.1
  9.1 0.2 collective-permute-start.3
  9.3 3.8 %collective-permute-start = (bf16[16,128,128]{2,1,0:T(8,128)(2,1)}, bf16[16,128,128]{2,1,0:T(8,128)(2,1)S(1)}, u32[]{:S(2)}, u32[]{:S(2)}) collective-permute-start(bf16[16,128,128]{2,1,0:T(8,128)(2,1)} %get-tuple-element.15), channel_id=1, source_target_pairs={{0,1},{2,3},{4,5},{6,7},{8,9},{10,11},{12,13},{14,15},{16,17},{18,... | collective-permute-start | bytes 1572872 | tf_op jit(solution)/shard_map/ppermute | solution.py:204
  13.1 2.0 %collective-permute-done.1 = bf16[4,128,128]{2,1,0:T(8,128)(2,1)S(1)} collective-permute-done((bf16[4,128,128]{2,1,0:T(8,128)(2,1)S(1)}, bf16[4,128,128]{2,1,0:T(8,128)(2,1)S(1)}, u32[]{:S(2)}, u32[]{:S(2)}) %collective-permute-start.1) | collective-permute-done | bytes 131104 | tf_op jit(solution)/shard_map/ppermute | solution.py:204
  15.1 0.0 collective-permute-done.3
  15.1 1.0 %fusion.2 = (bf16[4,128,128]{2,1,0:T(8,128)(2,1)S(1)}, f32[4,128,128]{2,1,0:T(8,128)S(1)}, bf16[4,128,128]{2,1,0:T(8,128)(2,1)S(1)}) fusion(bf16[4,128,128]{2,1,0:T(8,128)(2,1)S(1)} %collective-permute-done.2, bf16[4,128,128]{2,1,0:T(8,128)(2,1)S(1)} %collective-permute-done.1, bf16[4,128,128]{2,1,0:T(8,128)(2,1)S(1)} %collective-permute-done.3, ...), kind=kLoop, calls=%fused_computation.30 | loop fusion | flops 655360 | bytes 1048581 | tf_op jit(solution)/shard_map/convert_element_type | solution.py:219
  16.1 2.7 %collective-permute-start.6 = (bf16[4,128,128]{2,1,0:T(8,128)(2,1)S(1)}, bf16[4,128,128]{2,1,0:T(8,128)(2,1)S(1)}, u32[]{:S(2)}, u32[]{:S(2)}) collective-permute-start(bf16[4,128,128]{2,1,0:T(8,128)(2,1)S(1)} %get-tuple-element.19), channel_id=1, source_target_pairs={{0,4},{1,5},{2,6},{3,7},{4,0},{5,1},{6,2},{7,3},{8,12},{9,13},{10,... | collective-permute-start | bytes 393224 | tf_op jit(solution)/shard_map/ppermute | solution.py:204
  18.8 1.0 %slice_multiply_fusion = f32[5,16,512]{2,1,0:T(8,128)S(1)} fusion(f32[18,16,512]{2,1,0:T(8,128)} %w_ref.3, f32[5]{0:T(128)S(1)} %convert_multiply_fusion), kind=kLoop, calls=%fused_computation.16 | loop fusion | flops 40960 | bytes 327700 | tf_op jit(solution)/shard_map/mul | solution.py:259
  19.8 0.7 slice.8.w_ref
  20.4 0.6 stack.54.w_ref
  21.1 6.3 %shard_map.46 = (f32[16,128,256]{2,1,0:T(8,128)}, bf16[16,256,128]{2,1,0:T(8,128)(2,1)}) custom-call(bf16[512,16,128]{2,1,0:T(8,128)(2,1)} %q_ref.3, bf16[512,16,128]{2,1,0:T(8,128)(2,1)} %k_ref.5, bf16[512,16,128]{2,1,0:T(8,128)(2,1)} %v_ref.5, f32[18,16,512]{2,1,0:T(8,128)} %w_ref.3, bf16[16,128,128]{2,1,0:T(8,128)(2,1)} %get-tuple-element.11.first_ref), custom_call_target="tpu_custom_call" | custom-call | flops 536870912 | bytes 6291456 | tf_op jit(solution)/shard_map/pallas_call | solution.py:98
  27.3 4.4 %shard_map.47 = (f32[16,128,256]{2,1,0:T(8,128)}, bf16[16,256,128]{2,1,0:T(8,128)(2,1)}) custom-call(bf16[512,16,128]{2,1,0:T(8,128)(2,1)} %q_ref.3, bf16[512,16,128]{2,1,0:T(8,128)(2,1)} %k_ref.5, bf16[512,16,128]{2,1,0:T(8,128)(2,1)} %v_ref.5, f32[18,16,512]{2,1,0:T(8,128)} %w_ref.3, bf16[16,128,128]{2,1,0:T(8,128)(2,1)} %get-tuple-element.11.first_ref), custom_call_target="tpu_custom_call" | custom-call | flops 536870912 | bytes 6291456 | tf_op jit(solution)/shard_map/pallas_call | solution.py:98
  31.7 1.6 %collective-permute-start.4 = (bf16[4,128,128]{2,1,0:T(8,128)(2,1)S(1)}, bf16[4,128,128]{2,1,0:T(8,128)(2,1)S(1)}, u32[]{:S(2)}, u32[]{:S(2)}) collective-permute-start(bf16[4,128,128]{2,1,0:T(8,128)(2,1)S(1)} %get-tuple-element.21), channel_id=1, source_target_pairs={{0,2},{1,3},{2,0},{3,1},{4,6},{5,7},{6,4},{7,5},{8,10},{9,11},{10,... | collective-permute-start | bytes 393224 | tf_op jit(solution)/shard_map/ppermute | solution.py:204
  33.3 0.0 collective-permute-done.6
  33.4 0.1 collective-permute-start.9
  33.4 3.3 %collective-permute-done.4 = bf16[4,128,128]{2,1,0:T(8,128)(2,1)S(1)} collective-permute-done((bf16[4,128,128]{2,1,0:T(8,128)(2,1)S(1)}, bf16[4,128,128]{2,1,0:T(8,128)(2,1)S(1)}, u32[]{:S(2)}, u32[]{:S(2)}) %collective-permute-start.4) | collective-permute-done | bytes 131104 | tf_op jit(solution)/shard_map/ppermute | solution.py:204
  36.8 1.8 %collective-permute-start.5 = (bf16[2,4,128,128]{3,2,1,0:T(8,128)(2,1)S(1)}, bf16[2,4,128,128]{3,2,1,0:T(8,128)(2,1)S(1)}, u32[]{:S(2)}, u32[]{:S(2)}) collective-permute-start(bf16[2,4,128,128]{3,2,1,0:T(8,128)(2,1)S(1)} %pad_maximum_fusion.2), channel_id=1, source_target_pairs={{0,1},{1,0},{2,3},{3,2},{4,5},{5,4},{6,7},{7,6},{8,9},{9,8},{10,11... | collective-permute-start | bytes 786440 | tf_op jit(solution)/shard_map/ppermute | solution.py:204
  38.6 1.6 %collective-permute-start.7 = (bf16[4,128,128]{2,1,0:T(8,128)(2,1)S(1)}, bf16[4,128,128]{2,1,0:T(8,128)(2,1)S(1)}, u32[]{:S(2)}, u32[]{:S(2)}) collective-permute-start(bf16[4,128,128]{2,1,0:T(8,128)(2,1)S(1)} %collective-permute-done.6), channel_id=1, source_target_pairs={{0,2},{1,3},{2,0},{3,1},{4,6},{5,7},{6,4},{7,5},{8,10},{9,11},{10,... | collective-permute-start | bytes 393224 | tf_op jit(solution)/shard_map/ppermute | solution.py:204
  40.1 0.0 collective-permute-done.9
  40.1 0.1 add_convert_fusion
  40.2 1.6 %collective-permute-start.10 = (bf16[4,128,128]{2,1,0:T(8,128)(2,1)S(1)}, bf16[4,128,128]{2,1,0:T(8,128)(2,1)S(1)}, u32[]{:S(2)}, u32[]{:S(2)}) collective-permute-start(bf16[4,128,128]{2,1,0:T(8,128)(2,1)S(1)} %add_convert_fusion), channel_id=1, source_target_pairs={{0,16},{1,17},{2,18},{3,19},{4,20},{5,21},{6,22},{7,23},{8,24},{9,... | collective-permute-start | bytes 393224 | tf_op jit(solution)/shard_map/ppermute | solution.py:204
  41.8 1.7 %collective-permute-done.7 = bf16[4,128,128]{2,1,0:T(8,128)(2,1)S(1)} collective-permute-done((bf16[4,128,128]{2,1,0:T(8,128)(2,1)S(1)}, bf16[4,128,128]{2,1,0:T(8,128)(2,1)S(1)}, u32[]{:S(2)}, u32[]{:S(2)}) %collective-permute-start.7) | collective-permute-done | bytes 131104 | tf_op jit(solution)/shard_map/ppermute | solution.py:204
  43.6 0.4 collective-permute-start.8
  44.0 1.3 %collective-permute-done.10 = bf16[4,128,128]{2,1,0:T(8,128)(2,1)S(1)} collective-permute-done((bf16[4,128,128]{2,1,0:T(8,128)(2,1)S(1)}, bf16[4,128,128]{2,1,0:T(8,128)(2,1)S(1)}, u32[]{:S(2)}, u32[]{:S(2)}) %collective-permute-start.10) | collective-permute-done | bytes 131104 | tf_op jit(solution)/shard_map/ppermute | solution.py:204
  45.2 0.1 broadcast_in_dim.16
  45.3 0.1 bitcast_dynamic-update-slice_fusion.3
  45.4 1.5 %collective-permute-start.11 = (bf16[4,128,128]{2,1,0:T(8,128)(2,1)S(1)}, bf16[4,128,128]{2,1,0:T(8,128)(2,1)S(1)}, u32[]{:S(2)}, u32[]{:S(2)}) collective-permute-start(bf16[4,128,128]{2,1,0:T(8,128)(2,1)S(1)} %get-tuple-element.18), channel_id=1, source_target_pairs={{0,3},{1,2},{2,1},{3,0},{4,7},{5,6},{6,5},{7,4},{8,11},{9,10},{10,... | collective-permute-start | bytes 393224 | tf_op jit(solution)/shard_map/ppermute | solution.py:204
  47.0 0.4 collective-permute-start.12
  47.4 1.6 %collective-permute-start.13 = (bf16[4,128,128]{2,1,0:T(8,128)(2,1)S(1)}, bf16[4,128,128]{2,1,0:T(8,128)(2,1)S(1)}, u32[]{:S(2)}, u32[]{:S(2)}) collective-permute-start(bf16[4,128,128]{2,1,0:T(8,128)(2,1)S(1)} %get-tuple-element.18), channel_id=1, source_target_pairs={{0,1},{1,0},{2,3},{3,2},{4,5},{5,4},{6,7},{7,6},{8,9},{9,8},{10,11... | collective-permute-start | bytes 393224 | tf_op jit(solution)/shard_map/ppermute | solution.py:204
  49.0 2.4 %collective-permute-done.11 = bf16[4,128,128]{2,1,0:T(8,128)(2,1)S(1)} collective-permute-done((bf16[4,128,128]{2,1,0:T(8,128)(2,1)S(1)}, bf16[4,128,128]{2,1,0:T(8,128)(2,1)S(1)}, u32[]{:S(2)}, u32[]{:S(2)}) %collective-permute-start.11) | collective-permute-done | bytes 131104 | tf_op jit(solution)/shard_map/ppermute | solution.py:204
  51.5 0.4 collective-permute-done.12
  51.9 2.5 %collective-permute-done.13 = bf16[4,128,128]{2,1,0:T(8,128)(2,1)S(1)} collective-permute-done((bf16[4,128,128]{2,1,0:T(8,128)(2,1)S(1)}, bf16[4,128,128]{2,1,0:T(8,128)(2,1)S(1)}, u32[]{:S(2)}, u32[]{:S(2)}) %collective-permute-start.13) | collective-permute-done | bytes 131104 | tf_op jit(solution)/shard_map/ppermute | solution.py:204
  54.5 1.3 %collective-permute-start.14 = (bf16[16,128,128]{2,1,0:T(8,128)(2,1)S(1)}, bf16[16,128,128]{2,1,0:T(8,128)(2,1)S(1)}, u32[]{:S(2)}, u32[]{:S(2)}) collective-permute-start(bf16[16,128,128]{2,1,0:T(8,128)(2,1)S(1)} %bitcast.28), channel_id=1, source_target_pairs={{0,8},{1,9},{2,10},{3,11},{4,12},{5,13},{6,14},{7,15},{16,24},{17,... | collective-permute-start | bytes 1572872 | tf_op jit(solution)/shard_map/ppermute | solution.py:204
  55.8 0.1 pad_maximum_fusion
  55.9 0.8 %copy.7 = bf16[2,2,4,128,128]{4,3,2,1,0:T(8,128)(2,1)} copy(bf16[2,2,4,128,128]{4,3,2,0,1:T(8,128)(2,1)S(1)} %pad_maximum_fusion) | data formatting | bytes 1048576 | tf_op jit(solution)/shard_map/stack | solution.py:227
  56.7 0.0 collective-permute-done.8
  56.8 0.1 pad_maximum_fusion.1
  56.8 0.8 %copy.8 = bf16[2,2,4,128,128]{4,3,2,1,0:T(8,128)(2,1)} copy(bf16[2,2,4,128,128]{4,3,2,0,1:T(8,128)(2,1)S(1)} %pad_maximum_fusion.1) | data formatting | bytes 1048576 | tf_op jit(solution)/shard_map/stack | solution.py:227
  57.7 0.0 collective-permute-done.rest_0_
  57.7 0.8 %copy-done.1 = bf16[16,128,128]{2,1,0:T(8,128)(2,1)} copy-done((bf16[16,128,128]{2,1,0:T(8,128)(2,1)}, bf16[16,128,128]{2,1,0:T(8,128)(2,1)S(1)}, u32[]{:S(2)}) %copy-start.1) | copy-done | bytes 524312
  58.5 3.9 %shard_map.48.a0_ref = f32[16,128,256]{2,1,0:T(8,128)} custom-call(bf16[16,256,128]{2,1,0:T(8,128)(2,1)} %get-tuple-element.12.qh_ref.q0_ref, f32[16,128,256]{2,1,0:T(8,128)} %get-tuple-element.14.acc_ref, f32[3,16,512]{2,1,0:T(8,128)} %slice.8.w_ref, bf16[16,128,128]{2,1,0:T(8,128)(2,1)} %copy-done.1, ...), custom_call_target="tpu_custom_call", output_to_operand_aliasing={{}: (1, {})} | custom-call | flops 402653184 | bytes 5242880 | tf_op jit(solution)/shard_map/pallas_call | solution.py:136
  62.3 3.9 %shard_map.49.a1_ref = f32[16,128,256]{2,1,0:T(8,128)} custom-call(bf16[16,256,128]{2,1,0:T(8,128)(2,1)} %get-tuple-element.13.qh_ref.q1_ref, f32[16,128,256]{2,1,0:T(8,128)} %get-tuple-element.16.acc_ref, f32[3,16,512]{2,1,0:T(8,128)} %slice.8.w_ref, bf16[16,128,128]{2,1,0:T(8,128)(2,1)} %copy-done.1, ...), custom_call_target="tpu_custom_call", output_to_operand_aliasing={{}: (1, {})} | custom-call | flops 402653184 | bytes 5242880 | tf_op jit(solution)/shard_map/pallas_call | solution.py:136
  66.2 0.0 collective-permute-done.14
  66.2 0.9 %broadcast_select_fusion.rest_1_ = bf16[16,128,128]{2,1,0:T(8,128)(2,1)} fusion(bf16[16,128,128]{2,1,0:T(8,128)(2,1)S(1)} %collective-permute-done.14, pred[]{:T(512)S(6)} %eq.11, bf16[4,4,128,128]{3,2,1,0:T(8,128)(2,1)S(1)} %bitcast_dynamic-update-slice_fusion), kind=kLoop, calls=%fused_computation.2 | loop fusion | flops 262144 | bytes 1572865 | tf_op jit(solution)/shard_map/jit(_where)/select_n | solution.py:244
  67.1 6.2 %final.1 = bf16[512,16,128]{2,1,0:T(8,128)(2,1)} custom-call(bf16[16,256,128]{2,1,0:T(8,128)(2,1)} %get-tuple-element.12.qh_ref.q0_ref, bf16[16,256,128]{2,1,0:T(8,128)(2,1)} %get-tuple-element.13.qh_ref.q1_ref, f32[16,128,256]{2,1,0:T(8,128)} %shard_map.48.a0_ref, f32[16,128,256]{2,1,0:T(8,128)} %shard_map.49.a1_ref, f32[2,16,512]{2,1,0:T(8,128)} %stack.54.w_ref, ...), custom_call_target="tpu_custom_call" | custom-call | flops 536870912 | bytes 8388608 | tf_op jit(solution)/shard_map/final/pallas_call | solution.py:179
  (16 shorter events, 0.3 us)
Async XLA Ops:
  4.6 8.5 %collective-permute-start.2 = (bf16[4,128,128]{2,1,0:T(8,128)(2,1)S(1)}, bf16[4,128,128]{2,1,0:T(8,128)(2,1)S(1)}, u32[]{:S(2)}, u32[]{:S(2)}) collective-permute-start(bf16[4,128,128]{2,1,0:T(8,128)(2,1)S(1)} %get-tuple-element.27), channel_id=1, source_target_pairs={{0,3},{1,2},{2,1},{3,0},{4,7},{5,6},{6,5},{7,4},{8,11},{9,10},{10,... | collective-permute-start | bytes 393224 | tf_op jit(solution)/shard_map/ppermute | solution.py:204
  8.6 6.5 %collective-permute-start.1 = (bf16[4,128,128]{2,1,0:T(8,128)(2,1)S(1)}, bf16[4,128,128]{2,1,0:T(8,128)(2,1)S(1)}, u32[]{:S(2)}, u32[]{:S(2)}) collective-permute-start(bf16[4,128,128]{2,1,0:T(8,128)(2,1)S(1)} %get-tuple-element.28), channel_id=1, source_target_pairs={{0,2},{1,3},{2,0},{3,1},{4,6},{5,7},{6,4},{7,5},{8,10},{9,11},{10,... | collective-permute-start | bytes 393224 | tf_op jit(solution)/shard_map/ppermute | solution.py:204
  9.1 6.0 %collective-permute-start.3 = (bf16[4,128,128]{2,1,0:T(8,128)(2,1)S(1)}, bf16[4,128,128]{2,1,0:T(8,128)(2,1)S(1)}, u32[]{:S(2)}, u32[]{:S(2)}) collective-permute-start(bf16[4,128,128]{2,1,0:T(8,128)(2,1)S(1)} %get-tuple-element.26), channel_id=1, source_target_pairs={{0,1},{1,0},{2,3},{3,2},{4,5},{5,4},{6,7},{7,6},{8,9},{9,8},{10,11... | collective-permute-start | bytes 393224 | tf_op jit(solution)/shard_map/ppermute | solution.py:204
  9.3 48.4 %collective-permute-start = (bf16[16,128,128]{2,1,0:T(8,128)(2,1)}, bf16[16,128,128]{2,1,0:T(8,128)(2,1)S(1)}, u32[]{:S(2)}, u32[]{:S(2)}) collective-permute-start(bf16[16,128,128]{2,1,0:T(8,128)(2,1)} %get-tuple-element.15), channel_id=1, source_target_pairs={{0,1},{2,3},{4,5},{6,7},{8,9},{10,11},{12,13},{14,15},{16,17},{18,... | collective-permute-start | bytes 1572872 | tf_op jit(solution)/shard_map/ppermute | solution.py:204
  16.1 17.2 %collective-permute-start.6 = (bf16[4,128,128]{2,1,0:T(8,128)(2,1)S(1)}, bf16[4,128,128]{2,1,0:T(8,128)(2,1)S(1)}, u32[]{:S(2)}, u32[]{:S(2)}) collective-permute-start(bf16[4,128,128]{2,1,0:T(8,128)(2,1)S(1)} %get-tuple-element.19), channel_id=1, source_target_pairs={{0,4},{1,5},{2,6},{3,7},{4,0},{5,1},{6,2},{7,3},{8,12},{9,13},{10,... | collective-permute-start | bytes 393224 | tf_op jit(solution)/shard_map/ppermute | solution.py:204
  31.7 5.0 %collective-permute-start.4 = (bf16[4,128,128]{2,1,0:T(8,128)(2,1)S(1)}, bf16[4,128,128]{2,1,0:T(8,128)(2,1)S(1)}, u32[]{:S(2)}, u32[]{:S(2)}) collective-permute-start(bf16[4,128,128]{2,1,0:T(8,128)(2,1)S(1)} %get-tuple-element.21), channel_id=1, source_target_pairs={{0,2},{1,3},{2,0},{3,1},{4,6},{5,7},{6,4},{7,5},{8,10},{9,11},{10,... | collective-permute-start | bytes 393224 | tf_op jit(solution)/shard_map/ppermute | solution.py:204
  33.4 6.8 %collective-permute-start.9 = (bf16[4,128,128]{2,1,0:T(8,128)(2,1)S(1)}, bf16[4,128,128]{2,1,0:T(8,128)(2,1)S(1)}, u32[]{:S(2)}, u32[]{:S(2)}) collective-permute-start(bf16[4,128,128]{2,1,0:T(8,128)(2,1)S(1)} %fusion.1), channel_id=1, source_target_pairs={{0,8},{1,9},{2,10},{3,11},{4,12},{5,13},{6,14},{7,15},{8,0},{9,1},... | collective-permute-start | bytes 393224 | tf_op jit(solution)/shard_map/ppermute | solution.py:204
  36.8 10.6 %collective-permute-start.5 = (bf16[2,4,128,128]{3,2,1,0:T(8,128)(2,1)S(1)}, bf16[2,4,128,128]{3,2,1,0:T(8,128)(2,1)S(1)}, u32[]{:S(2)}, u32[]{:S(2)}) collective-permute-start(bf16[2,4,128,128]{3,2,1,0:T(8,128)(2,1)S(1)} %pad_maximum_fusion.2), channel_id=1, source_target_pairs={{0,1},{1,0},{2,3},{3,2},{4,5},{5,4},{6,7},{7,6},{8,9},{9,8},{10,11... | collective-permute-start | bytes 786440 | tf_op jit(solution)/shard_map/ppermute | solution.py:204
  38.6 5.0 %collective-permute-start.7 = (bf16[4,128,128]{2,1,0:T(8,128)(2,1)S(1)}, bf16[4,128,128]{2,1,0:T(8,128)(2,1)S(1)}, u32[]{:S(2)}, u32[]{:S(2)}) collective-permute-start(bf16[4,128,128]{2,1,0:T(8,128)(2,1)S(1)} %collective-permute-done.6), channel_id=1, source_target_pairs={{0,2},{1,3},{2,0},{3,1},{4,6},{5,7},{6,4},{7,5},{8,10},{9,11},{10,... | collective-permute-start | bytes 393224 | tf_op jit(solution)/shard_map/ppermute | solution.py:204
  40.2 5.0 %collective-permute-start.10 = (bf16[4,128,128]{2,1,0:T(8,128)(2,1)S(1)}, bf16[4,128,128]{2,1,0:T(8,128)(2,1)S(1)}, u32[]{:S(2)}, u32[]{:S(2)}) collective-permute-start(bf16[4,128,128]{2,1,0:T(8,128)(2,1)S(1)} %add_convert_fusion), channel_id=1, source_target_pairs={{0,16},{1,17},{2,18},{3,19},{4,20},{5,21},{6,22},{7,23},{8,24},{9,... | collective-permute-start | bytes 393224 | tf_op jit(solution)/shard_map/ppermute | solution.py:204
  43.6 13.1 %collective-permute-start.8 = (bf16[2,4,128,128]{3,2,1,0:T(8,128)(2,1)S(1)}, bf16[2,4,128,128]{3,2,1,0:T(8,128)(2,1)S(1)}, u32[]{:S(2)}, u32[]{:S(2)}) collective-permute-start(bf16[2,4,128,128]{3,2,1,0:T(8,128)(2,1)S(1)} %pad_maximum_fusion.3), channel_id=1, source_target_pairs={{0,1},{1,0},{2,3},{3,2},{4,5},{5,4},{6,7},{7,6},{8,9},{9,8},{10,11... | collective-permute-start | bytes 786440 | tf_op jit(solution)/shard_map/ppermute | solution.py:204
  45.4 6.0 %collective-permute-start.11 = (bf16[4,128,128]{2,1,0:T(8,128)(2,1)S(1)}, bf16[4,128,128]{2,1,0:T(8,128)(2,1)S(1)}, u32[]{:S(2)}, u32[]{:S(2)}) collective-permute-start(bf16[4,128,128]{2,1,0:T(8,128)(2,1)S(1)} %get-tuple-element.18), channel_id=1, source_target_pairs={{0,3},{1,2},{2,1},{3,0},{4,7},{5,6},{6,5},{7,4},{8,11},{9,10},{10,... | collective-permute-start | bytes 393224 | tf_op jit(solution)/shard_map/ppermute | solution.py:204
  47.0 5.0 %collective-permute-start.12 = (bf16[4,128,128]{2,1,0:T(8,128)(2,1)S(1)}, bf16[4,128,128]{2,1,0:T(8,128)(2,1)S(1)}, u32[]{:S(2)}, u32[]{:S(2)}) collective-permute-start(bf16[4,128,128]{2,1,0:T(8,128)(2,1)S(1)} %get-tuple-element.18), channel_id=1, source_target_pairs={{0,2},{1,3},{2,0},{3,1},{4,6},{5,7},{6,4},{7,5},{8,10},{9,11},{10,... | collective-permute-start | bytes 393224 | tf_op jit(solution)/shard_map/ppermute | solution.py:204
  47.4 7.1 %collective-permute-start.13 = (bf16[4,128,128]{2,1,0:T(8,128)(2,1)S(1)}, bf16[4,128,128]{2,1,0:T(8,128)(2,1)S(1)}, u32[]{:S(2)}, u32[]{:S(2)}) collective-permute-start(bf16[4,128,128]{2,1,0:T(8,128)(2,1)S(1)} %get-tuple-element.18), channel_id=1, source_target_pairs={{0,1},{1,0},{2,3},{3,2},{4,5},{5,4},{6,7},{7,6},{8,9},{9,8},{10,11... | collective-permute-start | bytes 393224 | tf_op jit(solution)/shard_map/ppermute | solution.py:204
  54.5 11.7 %copy-start = (bf16[4,4,128,128]{3,2,1,0:T(8,128)(2,1)}, bf16[4,4,128,128]{3,2,1,0:T(8,128)(2,1)S(1)}, u32[]{:S(2)}) copy-start(bf16[4,4,128,128]{3,2,1,0:T(8,128)(2,1)S(1)} %bitcast_dynamic-update-slice_fusion) | copy-start | bytes 1572868
  54.5 11.7 %collective-permute-start.14 = (bf16[16,128,128]{2,1,0:T(8,128)(2,1)S(1)}, bf16[16,128,128]{2,1,0:T(8,128)(2,1)S(1)}, u32[]{:S(2)}, u32[]{:S(2)}) collective-permute-start(bf16[16,128,128]{2,1,0:T(8,128)(2,1)S(1)} %bitcast.28), channel_id=1, source_target_pairs={{0,8},{1,9},{2,10},{3,11},{4,12},{5,13},{6,14},{7,15},{16,24},{17,... | collective-permute-start | bytes 1572872 | tf_op jit(solution)/shard_map/ppermute | solution.py:204
  57.7 0.8 %copy-start.1 = (bf16[16,128,128]{2,1,0:T(8,128)(2,1)}, bf16[16,128,128]{2,1,0:T(8,128)(2,1)S(1)}, u32[]{:S(2)}) copy-start(bf16[16,128,128]{2,1,0:T(8,128)(2,1)S(1)} %collective-permute-done.rest_0_) | copy-start | bytes 1572868

commit v2 on v1

v2 whole, which is shorter than its diff:
```python
import functools
import jax
import jax.numpy as jnp
from jax import lax
from jax.experimental import pallas as pl
from jax.experimental.pallas import tpu as pltpu
from jax.sharding import PartitionSpec as P

AXES = ("outer", "inner")
HEAD_BLOCK = 8
STATE_VMEM = 9 << 20
LOCAL_VMEM = 9 << 20
FINAL_VMEM = 12 << 20
F32, BF16 = jnp.float32, jnp.bfloat16


def dot_nt(a, b):
    return lax.dot_general(a, b, (((1,), (1,)), ((), ())), preferred_element_type=F32)


def scalar_grid(grid, in_specs, out_specs):
    return pltpu.PrefetchScalarGridSpec(
        num_scalar_prefetch=1, grid=grid, in_specs=in_specs, out_specs=out_specs
    )


def state_kernel(place_ref, k_ref, v_ref, state_ref, first_ref):
    half = k_ref.shape[0] // 2
    quarter = k_ref.shape[1] // 2
    flip = place_ref[0] & 1
    keys = jnp.swapaxes(k_ref[...], 0, 1)
    values = jnp.swapaxes(v_ref[...], 0, 1)
    for h in range(2 * quarter):
        turned = values[h].T
        first = jnp.dot(turned[:, :half], keys[h, :half], preferred_element_type=F32)
        rest = jnp.dot(turned[:, half:], keys[h, half:], preferred_element_type=F32)
        first_ref[h] = first.astype(BF16)
        state_ref[(h // quarter ^ flip) * quarter + h % quarter] = (first + rest).astype(BF16)


def block_states(place, key_vectors, value_vectors):
    tokens, heads, dim = key_vectors.shape
    block = heads // 2
    source = pl.BlockSpec((tokens, block, dim), lambda i, p: (0, i ^ (p[0] >> 1 & 1), 0))
    shape = jax.ShapeDtypeStruct((heads, dim, dim), BF16)
    return pl.pallas_call(
        state_kernel,
        grid_spec=scalar_grid(
            (2,),
            [source, source],
            [
                pl.BlockSpec((block, dim, dim), lambda i, p: (i, 0, 0)),
                pl.BlockSpec((block, dim, dim), lambda i, p: (i ^ (p[0] >> 1 & 1), 0, 0)),
            ],
        ),
        out_shape=[shape, shape],
        name="states",
        compiler_params=pltpu.CompilerParams(vmem_limit_bytes=STATE_VMEM),
        cost_estimate=pl.CostEstimate(
            flops=2 * tokens * heads * dim * dim,
            bytes_accessed=4 * tokens * heads * dim,
            transcendentals=0,
        ),
    )(place, key_vectors, value_vectors)


def local_kernel(second, q_ref, k_ref, v_ref, w_ref, first_ref, acc_ref, qh_ref):
    tile = q_ref.shape[0]
    depth = tile.bit_length() - 1
    groups = tile // 8
    queries = jnp.swapaxes(q_ref[...], 0, 1)
    keys = jnp.swapaxes(k_ref[...], 0, 1)
    values = jnp.swapaxes(v_ref[...], 0, 1)
    heads = queries.shape[0]
    lane = lax.broadcasted_iota(jnp.int32, (8, tile), 1)
    row = lax.broadcasted_iota(jnp.int32, (8, tile), 0)
    fine = (lane & 7) ^ row
    fine_ok = row <= (lane & 7)
    group_lane = lax.broadcasted_iota(jnp.int32, (groups, tile), 1) >> 3
    group_row = lax.broadcasted_iota(jnp.int32, (groups, tile), 0)
    coarse = jnp.where(group_row < group_lane, group_lane ^ group_row, 0)

    def gain(l, h):
        return w_ref[l, h : h + 1, :] * (2.0 ** (-0.5 * l))

    def weigh(h, scores):
        near = jnp.where(fine == 0, gain(0, h), 0.0)
        for l in range(1, 4):
            near = jnp.where((fine >> (l - 1)) == 1, gain(l, h), near)
        near = jnp.where(fine_ok, near, 0.0)
        far = jnp.zeros((groups, tile), F32)
        for l in range(4, depth + 1):
            far = jnp.where((coarse >> (l - 4)) == 1, gain(l, h), far)
        rows = []
        for g in range(0, groups, 2):
            pair = [
                jnp.where(
                    (lane >> 3) == g + i,
                    near,
                    jnp.broadcast_to(far[g + i : g + i + 1, :], (8, tile)),
                )
                * scores[8 * (g + i) : 8 * (g + i) + 8, :]
                for i in range(2)
            ]
            rows.append(jnp.concatenate(pair, axis=0).astype(BF16))
        return jnp.concatenate(rows, axis=0)

    scores, weights = {}, {}
    for h in range(heads + 2):
        if h < heads:
            scores[h] = dot_nt(keys[h], queries[h])
            qh_ref[h] = queries[h]
        if 0 <= h - 1 < heads:
            weights[h - 1] = weigh(h - 1, scores.pop(h - 1))
        if h - 2 >= 0:
            n = h - 2
            out = jnp.dot(values[n].T, weights.pop(n), preferred_element_type=F32)
            if second:
                out = out + gain(depth + 1, n) * dot_nt(first_ref[n], queries[n])
            acc_ref[n] = out


def local_part(half, queries, key_vectors, value_vectors, level_weights, first):
    tokens, heads, dim = queries.shape
    tile = tokens // 2
    levels = tile.bit_length() + 1
    source = pl.BlockSpec((tile, HEAD_BLOCK, dim), lambda i: (half, i, 0))
    return pl.pallas_call(
        functools.partial(local_kernel, half == 1),
        grid=(heads // HEAD_BLOCK,),
        in_specs=[
            source,
            source,
            source,
            pl.BlockSpec((levels, HEAD_BLOCK, tile), lambda i: (0, i, half)),
            pl.BlockSpec((HEAD_BLOCK, dim, dim), lambda i: (i, 0, 0)),
        ],
        out_specs=[
            pl.BlockSpec((HEAD_BLOCK, dim, tile), lambda i: (i, 0, 0)),
            pl.BlockSpec((HEAD_BLOCK, tile, dim), lambda i: (i, 0, 0)),
        ],
        out_shape=[
            pltpu.HBM((heads, dim, tile), F32),
            pltpu.HBM((heads, tile, dim), BF16),
        ],
        compiler_params=pltpu.CompilerParams(vmem_limit_bytes=LOCAL_VMEM),
        cost_estimate=pl.CostEstimate(
            flops=4 * tile * tile * heads * dim,
            bytes_accessed=12 * tile * heads * dim,
            transcendentals=0,
        ),
    )(queries, key_vectors, value_vectors, level_weights, first)


def bucket_sum(place, block, base, w_ref, q_ref, h, refs, rows):
    quarter = refs[0].shape[0] // 4
    spot = block * q_ref.shape[0] + h
    stack = [
        ref[(spot // quarter ^ (place & 3) ^ b) * quarter + spot % quarter]
        for ref, b in zip(refs, base)
    ]
    wide = dot_nt(jnp.concatenate(stack, axis=0), q_ref[h])
    dim = stack[0].shape[0]
    total = None
    for n, row in enumerate(rows):
        gain = sum(w_ref[l, h : h + 1, :] * c for l, c in row)
        part = wide[n * dim : (n + 1) * dim] * gain
        total = part if total is None else total + part
    return total


def final_kernel(meta, place_ref, q0_ref, q1_ref, a0_ref, a1_ref, w_ref, *rest):
    out_ref = rest[-1]
    refs = rest[:-1]
    base, local_depth, low, top = meta
    place = place_ref[0]
    bit = lambda g: (place >> g & 1).astype(F32)
    level = lambda g, c: (local_depth + 1 + g, c * 2.0 ** (-0.5 * (local_depth + 1 + g)))
    rows = [[level(g, bit(g))] for g in range(top) if g != low]
    rows.append([level(low, bit(low)), level(top, bit(top) * (1.0 - bit(low)))])
    rows.append([level(top, bit(top) * bit(low))])

    def side(q_ref, a_ref):
        done = []
        for h in range(q_ref.shape[0]):
            total = a_ref[h] + bucket_sum(
                place, pl.program_id(1), base, w_ref, q_ref, h, refs, rows
            )
            done.append(total.T.astype(BF16))
        out_ref[...] = jnp.swapaxes(jnp.stack(done), 0, 1)

    which = pl.program_id(0)
    pl.when(which == 0)(lambda: side(q0_ref, a0_ref))
    pl.when(which == 1)(lambda: side(q1_ref, a1_ref))


def final_part(place, turned, accs, level_weights, buckets, base, low, top):
    heads, tile, dim = turned[0].shape
    count = len(buckets)
    blocks = heads // HEAD_BLOCK
    first = lambda s, i, p: (jnp.where(s == 0, i, blocks - 1), 0, 0)
    last = lambda s, i, p: (jnp.where(s == 1, i, 0), 0, 0)
    return pl.pallas_call(
        functools.partial(final_kernel, (base, (2 * tile).bit_length() - 1, low, top)),
        grid_spec=scalar_grid(
            (2, blocks),
            [
                pl.BlockSpec((HEAD_BLOCK, tile, dim), first),
                pl.BlockSpec((HEAD_BLOCK, tile, dim), last),
                pl.BlockSpec((HEAD_BLOCK, dim, tile), first),
                pl.BlockSpec((HEAD_BLOCK, dim, tile), last),
                pl.BlockSpec(
                    (level_weights.shape[0], HEAD_BLOCK, tile), lambda s, i, p: (0, i, s)
                ),
            ]
            + [pl.BlockSpec((heads, dim, dim), lambda s, i, p: (0, 0, 0))] * count,
            pl.BlockSpec((tile, HEAD_BLOCK, dim), lambda s, i, p: (s, i, 0)),
        ),
        out_shape=jax.ShapeDtypeStruct((2 * tile, heads, dim), BF16),
        name="final",
        compiler_params=pltpu.CompilerParams(vmem_limit_bytes=FINAL_VMEM),
        cost_estimate=pl.CostEstimate(
            flops=4 * count * tile * heads * dim * dim,
            bytes_accessed=16 * tile * heads * dim,
            transcendentals=0,
        ),
    )(place, *turned, *accs, level_weights, *buckets)


def exchange(value, mask, keep=None):
    total = lax.axis_size("outer") * lax.axis_size("inner")
    pairs = [(i, i ^ mask) for i in range(total) if keep is None or keep(i ^ mask)]
    return lax.ppermute(value, AXES, pairs)


def exchange_states(state, place, inner_depth, depth):
    quarter = state.shape[0] // 4
    high = (place >> 1 & 1) == 1
    part = lambda m: state[m * quarter : (m + 1) * quarter]
    got = {m: exchange(part(m), m) for m in (3, 2, 1)}
    zero = exchange(state, 1, lambda d: d & 1 == 1)
    mine = part(0).astype(F32) + got[1].astype(F32)
    other = got[2].astype(F32) + got[3].astype(F32)
    total = mine + other
    sent = total.astype(BF16)
    pieces = {1: jnp.where(high, other, mine).astype(BF16)}
    pieces[1], sent, total = lax.optimization_barrier((pieces[1], sent, total))
    for g in range(2, depth):
        pieces[g] = exchange(sent, 1 << g)
        total = total + pieces[g].astype(F32)
        sent = total.astype(BF16)

    def gather_late(g):
        a = pieces[g]
        b = exchange(a, 2)
        twin = exchange(jnp.concatenate([a, b]), 1)
        return jnp.concatenate([a, twin[:quarter], b, twin[quarter:]])

    low, top = inner_depth, depth - 1
    buckets = [zero] + [gather_late(g) for g in range(1, top) if g != low]
    chosen = jnp.where((place >> low & 1) == 1, pieces[low], pieces[top])
    got = {m: exchange(chosen, m) for m in (3, 2, 1)}
    full = jnp.concatenate([chosen, got[1], got[2], got[3]])
    buckets.append(full)
    buckets.append(exchange(full, 1 << low, lambda d: d >> low & 1 == 1))
    return buckets


def per_device(queries, key_vectors, value_vectors, level_weights):
    inner_count = lax.axis_size("inner")
    inner_depth = inner_count.bit_length() - 1
    depth = inner_depth + lax.axis_size("outer").bit_length() - 1
    place = lax.axis_index("outer") * inner_count + lax.axis_index("inner")
    where = place.astype(jnp.int32).reshape(1)
    far = lambda x: pltpu.with_memory_space_constraint(x, pltpu.HBM)
    queries, key_vectors, value_vectors = map(far, (queries, key_vectors, value_vectors))
    state, first = block_states(where, key_vectors, value_vectors)
    buckets = exchange_states(state, place, inner_depth, depth)
    turned, accs = [], []
    for half in range(2):
        acc, flat = local_part(half, queries, key_vectors, value_vectors, level_weights, first)
        accs.append(pltpu.with_memory_space_constraint(acc, pltpu.HBM))
        turned.append(pltpu.with_memory_space_constraint(flat, pltpu.HBM))
    base = (1,) + (0,) * (len(buckets) - 1)
    return final_part(
        where, turned, accs, level_weights, buckets, base, inner_depth, depth - 1
    )


def solution(mesh):
    placed = P(AXES, None, None)
    return jax.shard_map(
        per_device,
        mesh=mesh,
        in_specs=(placed, placed, placed, P(None, None, AXES)),
        out_specs=placed,
        check_vma=False,
    )
```

time: 73.6 us -> 66.2 us (0.90)
  waiting for transfers between devices: 13.8 us -> 27.6 us
  Pallas kernels: 28.1 us -> 18.5 us
  local copies, waits for them, and re-layouts: 4.97 us -> 0.07 us
  starting transfers between devices: 22.9 us -> 19.2 us
  other arithmetic: 3.32 us -> 0.46 us
    ppermute x15, waiting for transfers between devices: 13.8 us -> 27.6 us  [exchange(): return lax.ppermute(value, AXES, pairs)]
    pallas_call x4 -> x2, Pallas kernels: 17.5 us -> 9.98 us  [the longest x1 7.19 us: final_part(): pl.pallas_call(functools.partial(final_kernel, (base, (2 * tile).bit_leng...]
    ppermute x15, starting transfers between devices: 22.9 us -> 19.2 us  [exchange(): return lax.ppermute(value, AXES, pairs)]
    another operation x3 -> x0, local copies, waits for them, and re-layouts: 2.3 us -> none  [the longest x2 1.67 us: gather_late(): jnp.stack([jnp.where(odd, twin, pair), jnp.where(odd, pair, twin)], 1)]
    pallas_call x2, Pallas kernels: 10.7 us -> 8.51 us  [local_part(): pl.pallas_call(functools.partial(local_kernel, half == 1), grid=(heads //...]
    dynamic_slice x1 -> x0, local copies, waits for them, and re-layouts: 1.06 us -> none  [exchange_states(): part = lambda r: lax.dynamic_slice_in_dim(state, r * quarter, quarter, 0)]
    mul x2 -> x0, other arithmetic: 1 us -> none  [the longest x1 1 us: per_device(): level_weights[local_depth + 1:local_depth + 1 + depth]]
    convert_element_type x3, other arithmetic: 1.08 us -> 0.19 us  [exchange_states(): sent = total.astype(BF16)]
  transfers between devices with their start and end apart: 15 -> 15, of which waited for: 7 -> 7; matrix products, arithmetic and copies ran while one was open for 8% -> 1% of each run, Pallas kernels for 25% -> 13%
where the time goes in v2:
time: 66.2 us; the launch traced here: 66 us
  waiting for transfers between devices  27.6 us (42%)
  starting transfers between devices  19.2 us (29%)
  Pallas kernels  18.5 us (28%)
    ppermute x15, waiting for transfers between devices, exchange(): return lax.ppermute(value, AXES, pairs)  27.6 us
    ppermute x15, starting transfers between devices, exchange(): return lax.ppermute(value, AXES, pairs)  19.2 us
    pallas_call x2, Pallas kernels, local_part(): pl.pallas_call(functools.partial(local_kernel, half == 1), grid=(heads //...  8.51 us
    pallas_call x1, Pallas kernels, final_part(): pl.pallas_call(functools.partial(final_kernel, (base, (2 * tile).bit_leng...  7.19 us
    pallas_call x1, Pallas kernels, block_states(): pl.pallas_call(state_kernel, grid_spec=scalar_grid((2,), [source, source]...  2.79 us
  transfers between devices with their start and end apart: 15, of which 7 were waited for; matrix products, arithmetic and copies ran while one was open for 1% of the time, Pallas kernels for 13%

profile of v2, /device:TPU:0, one launch (start us, length us, event | category | flops | bytes accessed | tf_op | source)
XLA Modules:
  0.0 66.0 jit_solution(249014362317109720)
XLA Ops:
  0.0 2.8 %states.1 = (bf16[16,128,128]{2,1,0:T(8,128)(2,1)S(1)}, bf16[16,128,128]{2,1,0:T(8,128)(2,1)S(1)}) custom-call(s32[1]{0:T(128)} %bitcast.place_ref, bf16[512,16,128]{2,1,0:T(8,128)(2,1)} %k_ref.5, bf16[512,16,128]{2,1,0:T(8,128)(2,1)} %v_ref.5), custom_call_target="tpu_custom_call" | custom-call | flops 268435456 | bytes 4194304 | tf_op jit(solution)/shard_map/states/pallas_call | solution.py:46
  2.8 0.0 copy-start
  2.8 3.0 %collective-permute-start.3 = (bf16[4,128,128]{2,1,0:T(8,128)(2,1)S(1)}, bf16[4,128,128]{2,1,0:T(8,128)(2,1)S(1)}, u32[]{:S(2)}, u32[]{:S(2)}) collective-permute-start(bf16[4,128,128]{2,1,0:T(8,128)(2,1)S(1)} %get-tuple-element.26), channel_id=1, source_target_pairs={{0,1},{1,0},{2,3},{3,2},{4,5},{5,4},{6,7},{7,6},{8,9},{9,8},{10,11... | collective-permute-start | bytes 393224 | tf_op jit(solution)/shard_map/ppermute | solution.py:233
  5.9 1.6 %collective-permute-start.2 = (bf16[4,128,128]{2,1,0:T(8,128)(2,1)S(1)}, bf16[4,128,128]{2,1,0:T(8,128)(2,1)S(1)}, u32[]{:S(2)}, u32[]{:S(2)}) collective-permute-start(bf16[4,128,128]{2,1,0:T(8,128)(2,1)S(1)} %get-tuple-element.27), channel_id=1, source_target_pairs={{0,3},{1,2},{2,1},{3,0},{4,7},{5,6},{6,5},{7,4},{8,11},{9,10},{10,... | collective-permute-start | bytes 393224 | tf_op jit(solution)/shard_map/ppermute | solution.py:233
  7.4 0.0 collective-permute-start.1
  7.5 4.0 %collective-permute-done.3 = bf16[4,128,128]{2,1,0:T(8,128)(2,1)S(1)} collective-permute-done((bf16[4,128,128]{2,1,0:T(8,128)(2,1)S(1)}, bf16[4,128,128]{2,1,0:T(8,128)(2,1)S(1)}, u32[]{:S(2)}, u32[]{:S(2)}) %collective-permute-start.3) | collective-permute-done | bytes 131104 | tf_op jit(solution)/shard_map/ppermute | solution.py:233
  11.4 1.7 %collective-permute-done.2 = bf16[4,128,128]{2,1,0:T(8,128)(2,1)S(1)} collective-permute-done((bf16[4,128,128]{2,1,0:T(8,128)(2,1)S(1)}, bf16[4,128,128]{2,1,0:T(8,128)(2,1)S(1)}, u32[]{:S(2)}, u32[]{:S(2)}) %collective-permute-start.2) | collective-permute-done | bytes 131104 | tf_op jit(solution)/shard_map/ppermute | solution.py:233
  13.2 0.4 collective-permute-done.1
  13.5 0.1 fusion.2
  13.6 2.8 %collective-permute-start.6 = (bf16[4,128,128]{2,1,0:T(8,128)(2,1)S(1)}, bf16[4,128,128]{2,1,0:T(8,128)(2,1)S(1)}, u32[]{:S(2)}, u32[]{:S(2)}) collective-permute-start(bf16[4,128,128]{2,1,0:T(8,128)(2,1)S(1)} %get-tuple-element.21), channel_id=1, source_target_pairs={{0,4},{1,5},{2,6},{3,7},{4,0},{5,1},{6,2},{7,3},{8,12},{9,13},{10,... | collective-permute-start | bytes 393224 | tf_op jit(solution)/shard_map/ppermute | solution.py:233
  16.4 5.4 %collective-permute-done.6 = bf16[4,128,128]{2,1,0:T(8,128)(2,1)S(1)} collective-permute-done((bf16[4,128,128]{2,1,0:T(8,128)(2,1)S(1)}, bf16[4,128,128]{2,1,0:T(8,128)(2,1)S(1)}, u32[]{:S(2)}, u32[]{:S(2)}) %collective-permute-start.6) | collective-permute-done | bytes 131104 | tf_op jit(solution)/shard_map/ppermute | solution.py:233
  21.9 0.1 collective-permute-start.9
  21.9 0.6 collective-permute-start.4
  22.5 0.7 %collective-permute-done.9 = bf16[4,128,128]{2,1,0:T(8,128)(2,1)S(1)} collective-permute-done((bf16[4,128,128]{2,1,0:T(8,128)(2,1)S(1)}, bf16[4,128,128]{2,1,0:T(8,128)(2,1)S(1)}, u32[]{:S(2)}, u32[]{:S(2)}) %collective-permute-start.9) | collective-permute-done | bytes 131104 | tf_op jit(solution)/shard_map/ppermute | solution.py:233
  23.3 0.1 add_convert_fusion
  23.3 1.4 %collective-permute-start.10 = (bf16[4,128,128]{2,1,0:T(8,128)(2,1)S(1)}, bf16[4,128,128]{2,1,0:T(8,128)(2,1)S(1)}, u32[]{:S(2)}, u32[]{:S(2)}) collective-permute-start(bf16[4,128,128]{2,1,0:T(8,128)(2,1)S(1)} %add_convert_fusion), channel_id=1, source_target_pairs={{0,16},{1,17},{2,18},{3,19},{4,20},{5,21},{6,22},{7,23},{8,24},{9,... | collective-permute-start | bytes 393224 | tf_op jit(solution)/shard_map/ppermute | solution.py:233
  24.8 0.0 copy-done
  24.8 4.3 %shard_map.47 = (f32[16,128,256]{2,1,0:T(8,128)}, bf16[16,256,128]{2,1,0:T(8,128)(2,1)}) custom-call(bf16[512,16,128]{2,1,0:T(8,128)(2,1)} %q_ref.3, bf16[512,16,128]{2,1,0:T(8,128)(2,1)} %k_ref.5, bf16[512,16,128]{2,1,0:T(8,128)(2,1)} %v_ref.5, f32[18,16,512]{2,1,0:T(8,128)S(1)} %copy-done, bf16[16,128,128]{2,1,0:T(8,128)(2,1)S(1)} %get-tuple-element.14.first_ref), custom_call_target="tpu_custom_call" | custom-call | flops 536870912 | bytes 6291456 | tf_op jit(solution)/shard_map/pallas_call | solution.py:128
  29.1 0.0 collective-permute-done.4
  29.1 1.6 %collective-permute-start.5 = (bf16[8,128,128]{2,1,0:T(8,128)(2,1)S(1)}, bf16[8,128,128]{2,1,0:T(8,128)(2,1)S(1)}, u32[]{:S(2)}, u32[]{:S(2)}) collective-permute-start(bf16[8,128,128]{2,1,0:T(8,128)(2,1)S(1)} %pad_maximum_fusion.3), channel_id=1, source_target_pairs={{0,1},{1,0},{2,3},{3,2},{4,5},{5,4},{6,7},{7,6},{8,9},{9,8},{10,11... | collective-permute-start | bytes 786440 | tf_op jit(solution)/shard_map/ppermute | solution.py:233
  30.7 0.8 %collective-permute-start.7 = (bf16[4,128,128]{2,1,0:T(8,128)(2,1)S(1)}, bf16[4,128,128]{2,1,0:T(8,128)(2,1)S(1)}, u32[]{:S(2)}, u32[]{:S(2)}) collective-permute-start(bf16[4,128,128]{2,1,0:T(8,128)(2,1)S(1)} %collective-permute-done.6), channel_id=1, source_target_pairs={{0,2},{1,3},{2,0},{3,1},{4,6},{5,7},{6,4},{7,5},{8,10},{9,11},{10,... | collective-permute-start | bytes 393224 | tf_op jit(solution)/shard_map/ppermute | solution.py:233
  31.4 0.0 collective-permute-done.10
  31.4 1.3 %collective-permute-start.13 = (bf16[4,128,128]{2,1,0:T(8,128)(2,1)S(1)}, bf16[4,128,128]{2,1,0:T(8,128)(2,1)S(1)}, u32[]{:S(2)}, u32[]{:S(2)}) collective-permute-start(bf16[4,128,128]{2,1,0:T(8,128)(2,1)S(1)} %broadcast_select_fusion), channel_id=1, source_target_pairs={{0,3},{1,2},{2,1},{3,0},{4,7},{5,6},{6,5},{7,4},{8,11},{9,10},{10,... | collective-permute-start | bytes 393224 | tf_op jit(solution)/shard_map/ppermute | solution.py:233
  32.7 0.8 %collective-permute-start.12 = (bf16[4,128,128]{2,1,0:T(8,128)(2,1)S(1)}, bf16[4,128,128]{2,1,0:T(8,128)(2,1)S(1)}, u32[]{:S(2)}, u32[]{:S(2)}) collective-permute-start(bf16[4,128,128]{2,1,0:T(8,128)(2,1)S(1)} %broadcast_select_fusion), channel_id=1, source_target_pairs={{0,2},{1,3},{2,0},{3,1},{4,6},{5,7},{6,4},{7,5},{8,10},{9,11},{10,... | collective-permute-start | bytes 393224 | tf_op jit(solution)/shard_map/ppermute | solution.py:233
  33.5 1.5 %collective-permute-start.11 = (bf16[4,128,128]{2,1,0:T(8,128)(2,1)S(1)}, bf16[4,128,128]{2,1,0:T(8,128)(2,1)S(1)}, u32[]{:S(2)}, u32[]{:S(2)}) collective-permute-start(bf16[4,128,128]{2,1,0:T(8,128)(2,1)S(1)} %broadcast_select_fusion), channel_id=1, source_target_pairs={{0,1},{1,0},{2,3},{3,2},{4,5},{5,4},{6,7},{7,6},{8,9},{9,8},{10,11... | collective-permute-start | bytes 393224 | tf_op jit(solution)/shard_map/ppermute | solution.py:233
  35.0 4.2 %shard_map.46 = (f32[16,128,256]{2,1,0:T(8,128)}, bf16[16,256,128]{2,1,0:T(8,128)(2,1)}) custom-call(bf16[512,16,128]{2,1,0:T(8,128)(2,1)} %q_ref.3, bf16[512,16,128]{2,1,0:T(8,128)(2,1)} %k_ref.5, bf16[512,16,128]{2,1,0:T(8,128)(2,1)} %v_ref.5, f32[18,16,512]{2,1,0:T(8,128)S(1)} %copy-done, bf16[16,128,128]{2,1,0:T(8,128)(2,1)S(1)} %get-tuple-element.14.first_ref), custom_call_target="tpu_custom_call" | custom-call | flops 536870912 | bytes 6291456 | tf_op jit(solution)/shard_map/pallas_call | solution.py:128
  39.2 0.0 collective-permute-done.7
  39.2 2.4 %collective-permute-start = (bf16[16,128,128]{2,1,0:T(8,128)(2,1)S(1)}, bf16[16,128,128]{2,1,0:T(8,128)(2,1)S(1)}, u32[]{:S(2)}, u32[]{:S(2)}) collective-permute-start(bf16[16,128,128]{2,1,0:T(8,128)(2,1)S(1)} %get-tuple-element.19), channel_id=1, source_target_pairs={{0,1},{2,3},{4,5},{6,7},{8,9},{10,11},{12,13},{14,15},{16,17},{18,... | collective-permute-start | bytes 1572872 | tf_op jit(solution)/shard_map/ppermute | solution.py:233
  41.7 0.0 collective-permute-done.13
  41.7 0.1 collective-permute-start.8
  41.8 0.0 collective-permute-done.12
  41.8 1.3 %collective-permute-done.11 = bf16[4,128,128]{2,1,0:T(8,128)(2,1)S(1)} collective-permute-done((bf16[4,128,128]{2,1,0:T(8,128)(2,1)S(1)}, bf16[4,128,128]{2,1,0:T(8,128)(2,1)S(1)}, u32[]{:S(2)}, u32[]{:S(2)}) %collective-permute-start.11) | collective-permute-done | bytes 131104 | tf_op jit(solution)/shard_map/ppermute | solution.py:233
  43.1 0.1 pad_maximum_fusion.2.rest_3_
  43.2 1.3 %collective-permute-start.14 = (bf16[16,128,128]{2,1,0:T(8,128)(2,1)S(1)}, bf16[16,128,128]{2,1,0:T(8,128)(2,1)S(1)}, u32[]{:S(2)}, u32[]{:S(2)}) collective-permute-start(bf16[16,128,128]{2,1,0:T(8,128)(2,1)S(1)} %pad_maximum_fusion.2.rest_3_), channel_id=1, source_target_pairs={{0,8},{1,9},{2,10},{3,11},{4,12},{5,13},{6,14},{7,15},{16,24},{17,... | collective-permute-start | bytes 1572872 | tf_op jit(solution)/shard_map/ppermute | solution.py:233
  44.5 0.0 collective-permute-done.5
  44.5 0.1 pad_maximum_fusion.rest_1_
  44.6 14.1 %collective-permute-done.8 = bf16[8,128,128]{2,1,0:T(8,128)(2,1)S(1)} collective-permute-done((bf16[8,128,128]{2,1,0:T(8,128)(2,1)S(1)}, bf16[8,128,128]{2,1,0:T(8,128)(2,1)S(1)}, u32[]{:S(2)}, u32[]{:S(2)}) %collective-permute-start.8) | collective-permute-done | bytes 262176 | tf_op jit(solution)/shard_map/ppermute | solution.py:233
  58.7 0.1 pad_maximum_fusion.1.rest_2_
  58.8 0.0 collective-permute-done.rest_0_
  58.8 0.0 collective-permute-done.14.rest_4_
  58.8 7.2 %final.1 = bf16[512,16,128]{2,1,0:T(8,128)(2,1)} custom-call(s32[1]{0:T(128)} %bitcast.place_ref, bf16[16,256,128]{2,1,0:T(8,128)(2,1)} %get-tuple-element.15.q0_ref, bf16[16,256,128]{2,1,0:T(8,128)(2,1)} %get-tuple-element.16.q1_ref, f32[16,128,256]{2,1,0:T(8,128)} %get-tuple-element.17.a0_ref, f32[16,128,256]{2,1,0:T(8,128)} %get-tuple-element.18.a1_ref, ...), custom_call_target="tpu_custom_call" | custom-call | flops 1342177280 | bytes 8388608 | tf_op jit(solution)/shard_map/final/pallas_call | solution.py:203
  (7 shorter events, 0.2 us)
Async XLA Ops:
  2.8 22.0 %copy-start = (f32[18,16,512]{2,1,0:T(8,128)S(1)}, f32[18,16,512]{2,1,0:T(8,128)}, u32[]{:S(2)}) copy-start(f32[18,16,512]{2,1,0:T(8,128)} %w_ref.5) | copy-start | bytes 1769476
  2.8 8.6 %collective-permute-start.3 = (bf16[4,128,128]{2,1,0:T(8,128)(2,1)S(1)}, bf16[4,128,128]{2,1,0:T(8,128)(2,1)S(1)}, u32[]{:S(2)}, u32[]{:S(2)}) collective-permute-start(bf16[4,128,128]{2,1,0:T(8,128)(2,1)S(1)} %get-tuple-element.26), channel_id=1, source_target_pairs={{0,1},{1,0},{2,3},{3,2},{4,5},{5,4},{6,7},{7,6},{8,9},{9,8},{10,11... | collective-permute-start | bytes 393224 | tf_op jit(solution)/shard_map/ppermute | solution.py:233
  5.9 7.3 %collective-permute-start.2 = (bf16[4,128,128]{2,1,0:T(8,128)(2,1)S(1)}, bf16[4,128,128]{2,1,0:T(8,128)(2,1)S(1)}, u32[]{:S(2)}, u32[]{:S(2)}) collective-permute-start(bf16[4,128,128]{2,1,0:T(8,128)(2,1)S(1)} %get-tuple-element.27), channel_id=1, source_target_pairs={{0,3},{1,2},{2,1},{3,0},{4,7},{5,6},{6,5},{7,4},{8,11},{9,10},{10,... | collective-permute-start | bytes 393224 | tf_op jit(solution)/shard_map/ppermute | solution.py:233
  7.4 6.1 %collective-permute-start.1 = (bf16[4,128,128]{2,1,0:T(8,128)(2,1)S(1)}, bf16[4,128,128]{2,1,0:T(8,128)(2,1)S(1)}, u32[]{:S(2)}, u32[]{:S(2)}) collective-permute-start(bf16[4,128,128]{2,1,0:T(8,128)(2,1)S(1)} %get-tuple-element.28), channel_id=1, source_target_pairs={{0,2},{1,3},{2,0},{3,1},{4,6},{5,7},{6,4},{7,5},{8,10},{9,11},{10,... | collective-permute-start | bytes 393224 | tf_op jit(solution)/shard_map/ppermute | solution.py:233
  13.6 8.2 %collective-permute-start.6 = (bf16[4,128,128]{2,1,0:T(8,128)(2,1)S(1)}, bf16[4,128,128]{2,1,0:T(8,128)(2,1)S(1)}, u32[]{:S(2)}, u32[]{:S(2)}) collective-permute-start(bf16[4,128,128]{2,1,0:T(8,128)(2,1)S(1)} %get-tuple-element.21), channel_id=1, source_target_pairs={{0,4},{1,5},{2,6},{3,7},{4,0},{5,1},{6,2},{7,3},{8,12},{9,13},{10,... | collective-permute-start | bytes 393224 | tf_op jit(solution)/shard_map/ppermute | solution.py:233
  21.9 1.4 %collective-permute-start.9 = (bf16[4,128,128]{2,1,0:T(8,128)(2,1)S(1)}, bf16[4,128,128]{2,1,0:T(8,128)(2,1)S(1)}, u32[]{:S(2)}, u32[]{:S(2)}) collective-permute-start(bf16[4,128,128]{2,1,0:T(8,128)(2,1)S(1)} %fusion.1), channel_id=1, source_target_pairs={{0,8},{1,9},{2,10},{3,11},{4,12},{5,13},{6,14},{7,15},{8,0},{9,1},... | collective-permute-start | bytes 393224 | tf_op jit(solution)/shard_map/ppermute | solution.py:233
  21.9 7.1 %collective-permute-start.4 = (bf16[4,128,128]{2,1,0:T(8,128)(2,1)S(1)}, bf16[4,128,128]{2,1,0:T(8,128)(2,1)S(1)}, u32[]{:S(2)}, u32[]{:S(2)}) collective-permute-start(bf16[4,128,128]{2,1,0:T(8,128)(2,1)S(1)} %get-tuple-element.20), channel_id=1, source_target_pairs={{0,2},{1,3},{2,0},{3,1},{4,6},{5,7},{6,4},{7,5},{8,10},{9,11},{10,... | collective-permute-start | bytes 393224 | tf_op jit(solution)/shard_map/ppermute | solution.py:233
  23.3 8.1 %collective-permute-start.10 = (bf16[4,128,128]{2,1,0:T(8,128)(2,1)S(1)}, bf16[4,128,128]{2,1,0:T(8,128)(2,1)S(1)}, u32[]{:S(2)}, u32[]{:S(2)}) collective-permute-start(bf16[4,128,128]{2,1,0:T(8,128)(2,1)S(1)} %add_convert_fusion), channel_id=1, source_target_pairs={{0,16},{1,17},{2,18},{3,19},{4,20},{5,21},{6,22},{7,23},{8,24},{9,... | collective-permute-start | bytes 393224 | tf_op jit(solution)/shard_map/ppermute | solution.py:233
  29.1 15.4 %collective-permute-start.5 = (bf16[8,128,128]{2,1,0:T(8,128)(2,1)S(1)}, bf16[8,128,128]{2,1,0:T(8,128)(2,1)S(1)}, u32[]{:S(2)}, u32[]{:S(2)}) collective-permute-start(bf16[8,128,128]{2,1,0:T(8,128)(2,1)S(1)} %pad_maximum_fusion.3), channel_id=1, source_target_pairs={{0,1},{1,0},{2,3},{3,2},{4,5},{5,4},{6,7},{7,6},{8,9},{9,8},{10,11... | collective-permute-start | bytes 786440 | tf_op jit(solution)/shard_map/ppermute | solution.py:233
  30.7 8.6 %collective-permute-start.7 = (bf16[4,128,128]{2,1,0:T(8,128)(2,1)S(1)}, bf16[4,128,128]{2,1,0:T(8,128)(2,1)S(1)}, u32[]{:S(2)}, u32[]{:S(2)}) collective-permute-start(bf16[4,128,128]{2,1,0:T(8,128)(2,1)S(1)} %collective-permute-done.6), channel_id=1, source_target_pairs={{0,2},{1,3},{2,0},{3,1},{4,6},{5,7},{6,4},{7,5},{8,10},{9,11},{10,... | collective-permute-start | bytes 393224 | tf_op jit(solution)/shard_map/ppermute | solution.py:233
  31.4 10.3 %collective-permute-start.13 = (bf16[4,128,128]{2,1,0:T(8,128)(2,1)S(1)}, bf16[4,128,128]{2,1,0:T(8,128)(2,1)S(1)}, u32[]{:S(2)}, u32[]{:S(2)}) collective-permute-start(bf16[4,128,128]{2,1,0:T(8,128)(2,1)S(1)} %broadcast_select_fusion), channel_id=1, source_target_pairs={{0,3},{1,2},{2,1},{3,0},{4,7},{5,6},{6,5},{7,4},{8,11},{9,10},{10,... | collective-permute-start | bytes 393224 | tf_op jit(solution)/shard_map/ppermute | solution.py:233
  32.7 9.1 %collective-permute-start.12 = (bf16[4,128,128]{2,1,0:T(8,128)(2,1)S(1)}, bf16[4,128,128]{2,1,0:T(8,128)(2,1)S(1)}, u32[]{:S(2)}, u32[]{:S(2)}) collective-permute-start(bf16[4,128,128]{2,1,0:T(8,128)(2,1)S(1)} %broadcast_select_fusion), channel_id=1, source_target_pairs={{0,2},{1,3},{2,0},{3,1},{4,6},{5,7},{6,4},{7,5},{8,10},{9,11},{10,... | collective-permute-start | bytes 393224 | tf_op jit(solution)/shard_map/ppermute | solution.py:233
  33.5 9.6 %collective-permute-start.11 = (bf16[4,128,128]{2,1,0:T(8,128)(2,1)S(1)}, bf16[4,128,128]{2,1,0:T(8,128)(2,1)S(1)}, u32[]{:S(2)}, u32[]{:S(2)}) collective-permute-start(bf16[4,128,128]{2,1,0:T(8,128)(2,1)S(1)} %broadcast_select_fusion), channel_id=1, source_target_pairs={{0,1},{1,0},{2,3},{3,2},{4,5},{5,4},{6,7},{7,6},{8,9},{9,8},{10,11... | collective-permute-start | bytes 393224 | tf_op jit(solution)/shard_map/ppermute | solution.py:233
  39.2 19.6 %collective-permute-start = (bf16[16,128,128]{2,1,0:T(8,128)(2,1)S(1)}, bf16[16,128,128]{2,1,0:T(8,128)(2,1)S(1)}, u32[]{:S(2)}, u32[]{:S(2)}) collective-permute-start(bf16[16,128,128]{2,1,0:T(8,128)(2,1)S(1)} %get-tuple-element.19), channel_id=1, source_target_pairs={{0,1},{2,3},{4,5},{6,7},{8,9},{10,11},{12,13},{14,15},{16,17},{18,... | collective-permute-start | bytes 1572872 | tf_op jit(solution)/shard_map/ppermute | solution.py:233
  41.7 17.0 %collective-permute-start.8 = (bf16[8,128,128]{2,1,0:T(8,128)(2,1)S(1)}, bf16[8,128,128]{2,1,0:T(8,128)(2,1)S(1)}, u32[]{:S(2)}, u32[]{:S(2)}) collective-permute-start(bf16[8,128,128]{2,1,0:T(8,128)(2,1)S(1)} %pad_maximum_fusion.4), channel_id=1, source_target_pairs={{0,1},{1,0},{2,3},{3,2},{4,5},{5,4},{6,7},{7,6},{8,9},{9,8},{10,11... | collective-permute-start | bytes 786440 | tf_op jit(solution)/shard_map/ppermute | solution.py:233
  43.2 15.7 %collective-permute-start.14 = (bf16[16,128,128]{2,1,0:T(8,128)(2,1)S(1)}, bf16[16,128,128]{2,1,0:T(8,128)(2,1)S(1)}, u32[]{:S(2)}, u32[]{:S(2)}) collective-permute-start(bf16[16,128,128]{2,1,0:T(8,128)(2,1)S(1)} %pad_maximum_fusion.2.rest_3_), channel_id=1, source_target_pairs={{0,8},{1,9},{2,10},{3,11},{4,12},{5,13},{6,14},{7,15},{16,24},{17,... | collective-permute-start | bytes 1572872 | tf_op jit(solution)/shard_map/ppermute | solution.py:233
